TPU v7x, 256 devices: a whole 4x4x8 slice. The times are simulated.
256 devices in a mesh: span: 8 (over y_hi, x), wall: 32 (over y_lo, z, core).
Axes of the slice: x: 4, y: 4 (y_hi: 2, y_lo: 2; y = y_hi * 2 + y_lo), z: 8, core: 2. Of those that a mesh axis runs over, the one named last changes fastest.
Arguments:
- forcing: bfloat16 [2, 5, 4, 128, 128, 128], P(None, None, None, 'span', 'wall'), may hold values from -6 to 6
- span_factor: float32 [2, 5, 128], replicated, may hold values from -1 to 1
- pivot_inverse: bfloat16 [2, 5, 5, 128, 128, 128], P(None, None, None, 'span', 'wall'), may hold values from -0.046875 to 0.046875
- step_lower: bfloat16 [2, 5, 5, 128, 128, 128], P(None, None, None, 'span', 'wall'), may hold values from -1 to 1
- step_upper: bfloat16 [2, 5, 5, 128, 128, 128], P(None, None, None, 'span', 'wall'), may hold values from -1 to 1
Outputs:
- response: float32 [2, 5, 4, 128, 128, 128], P(None, None, None, 'span', 'wall')
All inputs are finite; a program needn't handle non-finite values.
Results may differ from a plain program's by a relative error of at most 0.0003.
Values may be sent and summed in bfloat16 or wider, within the bound.
A program may use at most 128 MiB of HBM per device.

v0:
```python
import math

import jax
import jax.numpy as jnp
from jax import lax
from jax.sharding import PartitionSpec as P

exact_mode = lax.Precision.HIGHEST


def entering(x, axis, combine, identity, reverse):
    size, here = (lax.axis_size(axis), lax.axis_index(axis))
    everything = jax.tree.map(lambda part: lax.all_gather(part, axis), x)
    start = jax.tree.map(
        lambda part, zero: jnp.broadcast_to(jnp.asarray(zero, part.dtype), part.shape), x, identity
    )

    def lap(k, before):
        at = size - 1 - k if reverse else k
        reached = at > here if reverse else at < here
        new = combine(before, jax.tree.map(lambda part: part[at], everything))
        return jax.tree.map(lambda a, b: jnp.where(reached, a, b), new, before)

    return lax.fori_loop(0, size, lap, start)


def small_product(matrix, vector):
    left_re = matrix[0][:, :, None]
    left_im = matrix[1][:, :, None]
    right_re = vector[0][None]
    right_im = vector[1][None]
    real = jnp.sum(left_re * right_re - left_im * right_im, axis=1)
    imag = jnp.sum(left_re * right_im + left_im * right_re, axis=1)
    return jnp.stack([real, imag])


def block_vector(matrix, vector):
    return small_product(matrix, vector)


def block_matrix(left, right):
    return small_product(left, right)


def compose_maps(earlier, later):
    return (block_matrix(later[0], earlier[0]), block_vector(later[0], earlier[1]) + later[1])


def span_kernel(span_factor, points):
    count = span_factor.shape[2]
    modes = jnp.arange(count, dtype=jnp.int32)
    scale = 2.0 * math.pi / count
    angle_points = (points[:, None] * modes[None, :] % count).astype(jnp.float32) * scale
    angle_modes = (modes[:, None] * modes[None, :] % count).astype(jnp.float32) * scale
    cos_points = jnp.cos(angle_points)[None]
    sin_points = jnp.sin(angle_points)[None]
    factor_re = span_factor[0][:, None, :]
    factor_im = span_factor[1][:, None, :]
    left_re = factor_re * cos_points - factor_im * sin_points
    left_im = factor_re * sin_points + factor_im * cos_points
    cos_modes = jnp.cos(angle_modes)
    sin_modes = jnp.sin(angle_modes)
    kernel_re = (
        jnp.einsum("crk,kw->crw", left_re, cos_modes, precision=exact_mode)
        + jnp.einsum("crk,kw->crw", left_im, sin_modes, precision=exact_mode)
    ) / count
    kernel_im = (
        jnp.einsum("crk,kw->crw", left_im, cos_modes, precision=exact_mode)
        - jnp.einsum("crk,kw->crw", left_re, sin_modes, precision=exact_mode)
    ) / count
    return (kernel_re, kernel_im)


def apply_kernel(kernel_re, kernel_im, lines):
    real = jnp.einsum("czw,cqwyx->cqzyx", kernel_re, lines[0], precision=exact_mode) - jnp.einsum(
        "czw,cqwyx->cqzyx", kernel_im, lines[1], precision=exact_mode
    )
    imag = jnp.einsum("czw,cqwyx->cqzyx", kernel_re, lines[1], precision=exact_mode) + jnp.einsum(
        "czw,cqwyx->cqzyx", kernel_im, lines[0], precision=exact_mode
    )
    return jnp.stack([real, imag])


def forward_entry(transfer, offset, identity):
    summary = entering(
        (transfer, offset), "wall", compose_maps, (identity, jnp.zeros_like(offset)), False
    )
    return summary[1]


def backward_entry(transfer, offset, identity):
    summary = entering(
        (transfer, offset), "wall", compose_maps, (identity, jnp.zeros_like(offset)), True
    )
    return summary[1]


def row_of(array, height):
    return lax.dynamic_index_in_dim(array, height, 4, False)


def local(forcing, span_factor, pivot_inverse, step_lower, step_upper):
    span_count = forcing.shape[3]
    own_points = lax.axis_index("span") * span_count + jnp.arange(span_count, dtype=jnp.int32)
    kernel_re, kernel_im = span_kernel(span_factor, own_points)
    driving = apply_kernel(
        kernel_re,
        kernel_im,
        lax.all_gather(forcing, "span", axis=3, tiled=True).astype(jnp.float32),
    )
    fields = forcing.shape[1]
    plane = (forcing.shape[3], forcing.shape[5])
    unit = jnp.broadcast_to(
        jnp.eye(fields, dtype=jnp.float32)[:, :, None, None], (fields, fields) + plane
    )
    identity = jnp.stack([unit, jnp.zeros_like(unit)])
    heights = jnp.arange(forcing.shape[4], dtype=jnp.int32)
    vector_zero = jnp.zeros(forcing.shape[:3] + plane, jnp.float32)

    def local_forward(state, height):
        offset, transfer = state
        lower = row_of(step_lower, height).astype(jnp.float32)
        source = block_vector(
            row_of(pivot_inverse, height).astype(jnp.float32), row_of(driving, height)
        )
        return ((source - block_vector(lower, offset), -block_matrix(lower, transfer)), source)

    (offset_low, transfer_low), sources = lax.scan(local_forward, (vector_zero, identity), heights)
    incoming = forward_entry(transfer_low, offset_low, identity)

    def sweep_step(previous, inputs):
        height, source = inputs
        lower = row_of(step_lower, height).astype(jnp.float32)
        current = source - block_vector(lower, previous)
        return (current, current)

    sweeps = lax.scan(sweep_step, incoming, (heights, sources))[1]

    def local_backward(state, inputs):
        offset, transfer = state
        height, sweep = inputs
        upper = row_of(step_upper, height).astype(jnp.float32)
        return ((sweep - block_vector(upper, offset), -block_matrix(upper, transfer)), None)

    (offset_up, transfer_up), unused = lax.scan(
        local_backward, (vector_zero, identity), (heights, sweeps), reverse=True
    )
    arriving = backward_entry(transfer_up, offset_up, identity)

    def answer_step(following, inputs):
        height, sweep = inputs
        upper = row_of(step_upper, height).astype(jnp.float32)
        current = sweep - block_vector(upper, following)
        return (current, current)

    answers = lax.scan(answer_step, arriving, (heights, sweeps), reverse=True)[1]
    return jnp.moveaxis(answers, 0, 4)


def solution(mesh):
    placed = (
        P(None, None, None, "span", "wall", None),
        P(),
        P(None, None, None, "span", "wall", None),
        P(None, None, None, "span", "wall", None),
        P(None, None, None, "span", "wall", None),
    )
    return jax.shard_map(
        local,
        mesh=mesh,
        in_specs=placed,
        out_specs=P(None, None, None, "span", "wall", None),
        check_vma=False,
    )
```

profile of v0, /device:TPU:1, one launch (start us, length us, event | category | flops | bytes accessed | tf_op | source)
XLA Modules:
  0.0 709.8 jit_solution(1325987464116603467)
XLA Ops:
  6.5 2.0 copy.21
  13.2 93.4 %all-gather.10.cloned.1.call-done = bf16[2,5,4,128,4,128]{5,3,4,2,1,0:T(8,128)(2,1)} async-done(((bf16[2,5,4,16,4,128]{5,3,4,2,1,0:T(8,128)(2,1)}), bf16[2,5,4,128,4,128]{5,3,4,2,1,0:T(8,128)(2,1)}) %all-gather.10.cloned.1.call-update) | async-done | bytes 5242896 | tf_op jit(solution)/shard_map/all_gather | solution.py:109
  106.6 3.0 fusion.3
  109.7 2.9 fusion.4
  112.6 1.1 fusion.10
  113.7 1.1 fusion.8
  114.8 1.2 pad_maximum_fusion.1
  116.0 1.2 broadcast.91.clone.1
  117.2 25.3 %while.92 = (s32[]{:T(128)}, f32[2,5,4,16,128]{4,3,2,1,0:T(8,128)S(1)}, f32[2,5,5,16,128]{4,3,2,1,0:T(8,128)S(1)}, f32[4,2,5,4,16,128]{5,4,3,2,1,0:T(8,128)}, s3...) while((s32[]{:T(128)}, ...), condition=%wide.region_7.8_spmd.clone, body=%wide.region_0.7_spmd.clone.sunk | while | flops 5877766 | bytes 12124845 | solution.py:128
  144.1 1.3 copy.26
  145.4 73.1 %all-gather.14.cloned.1.call-done = f32[64,5,4,16,128]{4,3,2,1,0:T(8,128)} async-done(((f32[2,5,4,16,128]{4,3,2,1,0:T(8,128)}), f32[64,5,4,16,128]{4,3,2,1,0:T(8,128)}) %all-gather.14.cloned.1.call-update) | async-done | bytes 10485776 | tf_op jit(solution)/shard_map/all_gather | solution.py:13
  218.5 83.4 %all-gather.12.cloned.1.call-done = f32[64,5,5,16,128]{4,3,2,1,0:T(8,128)} async-done(((f32[2,5,5,16,128]{4,3,2,1,0:T(8,128)}), f32[64,5,5,16,128]{4,3,2,1,0:T(8,128)}) %all-gather.12.cloned.1.call-update) | async-done | bytes 13107216 | tf_op jit(solution)/shard_map/all_gather | solution.py:13
  301.9 79.4 %while.93 = (s32[]{:T(128)}, f32[2,5,4,16,128]{4,3,2,1,0:T(8,128)S(1)}, s32[]{:T(128)}, f32[32,2,5,5,16,128]{5,4,3,2,1,0:T(8,128)}, f32[32,2,5,4,16,128]{5,4,3,2,1,0:T(8,128)}, /*index=5*/s32[]{:T(128)}, s32[]{:T(128)}, s32[]{}) while((s32[]{:T(128)}, f32[2,5,4,16,128]{4,3,2,1,0:T(8,128)S(1)}, s32[]{:T(128)}, ...), condition=%wide.region_11.12_spmd.clone, body=%wide.region_8.11_spmd.clone.sunk | while | flops 1966085 | bytes 4505730 | solution.py:24
  381.5 19.6 %while.90 = (s32[]{:T(128)}, f32[2,5,4,16,128]{4,3,2,1,0:T(8,128)S(1)}, f32[4,2,5,4,16,128]{5,4,3,2,1,0:T(8,128)S(1)}, f32[4,2,5,4,16,128]{5,4,3,2,1,0:T(8,128)}...) while((s32[]{:T(128)}, ...), condition=%wide.region_15.16_spmd, body=%wide.region_12.15_spmd.sunk | while | flops 1986565 | bytes 10363059 | solution.py:137
  401.2 13.5 %while.94 = (s32[]{:T(128)}, f32[2,5,4,16,128]{4,3,2,1,0:T(8,128)S(1)}, f32[2,5,5,16,128]{4,3,2,1,0:T(8,128)S(1)}, f32[4,2,5,4,16,128]{5,4,3,2,1,0:T(8,128)S(1)}...) while((s32[]{:T(128)}, ...), condition=%wide.region_21.22_spmd.clone, body=%wide.region_16.21_spmd.clone.sunk | while | flops 4055047 | bytes 7659697 | solution.py:145
  416.0 74.9 %all-gather.18.cloned.1.call-done = f32[64,5,4,16,128]{4,3,2,1,0:T(8,128)} async-done(((f32[2,5,4,16,128]{4,3,2,1,0:T(8,128)}), f32[64,5,4,16,128]{4,3,2,1,0:T(8,128)}) %all-gather.18.cloned.1.call-update) | async-done | bytes 10485776 | tf_op jit(solution)/shard_map/all_gather | solution.py:13
  490.8 83.2 %all-gather.16.cloned.1.call-done = f32[64,5,5,16,128]{4,3,2,1,0:T(8,128)} async-done(((f32[2,5,5,16,128]{4,3,2,1,0:T(8,128)}), f32[64,5,5,16,128]{4,3,2,1,0:T(8,128)}) %all-gather.16.cloned.1.call-update) | async-done | bytes 13107216 | tf_op jit(solution)/shard_map/all_gather | solution.py:13
  574.1 79.4 %while.95 = (s32[]{:T(128)}, f32[2,5,4,16,128]{4,3,2,1,0:T(8,128)S(1)}, s32[]{:T(128)}, f32[32,2,5,5,16,128]{5,4,3,2,1,0:T(8,128)}, f32[32,2,5,4,16,128]{5,4,3,2...) while((s32[]{:T(128)}, f32[2,5,4,16,128]{4,3,2,1,0:T(8,128)S(1)}, ...), condition=%wide.region_25.26_spmd.clone, body=%wide.region_22.25_spmd.clone.sunk | while | flops 1966089 | bytes 4505792 | solution.py:24
  575.4 1.1 fusion.84
  577.9 1.1 fusion.84
  580.4 1.1 fusion.84
  582.9 1.1 fusion.84
  585.3 1.1 fusion.84
  587.8 1.1 fusion.84
  590.3 1.1 fusion.84
  592.8 1.1 fusion.84
  595.3 1.1 fusion.84
  597.8 1.1 fusion.84
  600.2 1.1 fusion.84
  602.7 1.1 fusion.84
  605.2 1.1 fusion.84
  607.7 1.1 fusion.84
  610.2 1.1 fusion.84
  612.7 1.1 fusion.84
  617.6 1.1 fusion.84
  620.1 1.1 fusion.84
  622.6 1.1 fusion.84
  625.1 1.1 fusion.84
  627.5 1.1 fusion.84
  630.0 1.1 fusion.84
  632.5 1.1 fusion.84
  635.0 1.1 fusion.84
  653.5 1.4 broadcast.91.clone
  654.9 48.4 %while.91 = (s32[]{:T(128)}, f32[2,5,4,16,128]{4,3,2,1,0:T(8,128)S(1)}, f32[4,2,5,4,16,128]{5,0,4,3,2,1:T(4,128)}, f32[4,2,5,4,16,128]{5,4,3,2,1,0:T(8,128)S(1)}...) while((s32[]{:T(128)}, ...), condition=%wide.region_29.30_spmd, body=%wide.region_26.29_spmd.sunk | while | flops 1986566 | bytes 5775535 | solution.py:156
  657.8 9.1 %dynamic_update_slice.23 = f32[4,2,5,4,16,128]{5,0,4,3,2,1:T(4,128)} dynamic-update-slice(f32[4,2,5,4,16,128]{5,0,4,3,2,1:T(4,128)} %get-tuple-element.1307, f32[1,2,5,4,16,128]{5,0,4,3,2,1:T(1,128)S(1)} %bitcast.272, s32[]{:T(128)S(6)} %sub.195, s32[]{:T(128)} %constant.243.clone.1..sunk.1, s32[]{:T(128)} %constant.243.clone.1..sunk.1, s32[]{:T(128)} %constant.243.clone.1..sunk.1, ...) | dynamic-update-slice | bytes 655364 | tf_op jit(solution)/shard_map/while/body/jit(dynamic_update_index_in_dim)/dynamic_update_slice | solution.py:128
  669.9 9.1 %dynamic_update_slice.23 = f32[4,2,5,4,16,128]{5,0,4,3,2,1:T(4,128)} dynamic-update-slice(f32[4,2,5,4,16,128]{5,0,4,3,2,1:T(4,128)} %get-tuple-element.1307, f32[1,2,5,4,16,128]{5,0,4,3,2,1:T(1,128)S(1)} %bitcast.272, s32[]{:T(128)S(6)} %sub.195, s32[]{:T(128)} %constant.243.clone.1..sunk.1, s32[]{:T(128)} %constant.243.clone.1..sunk.1, s32[]{:T(128)} %constant.243.clone.1..sunk.1, ...) | dynamic-update-slice | bytes 655364 | tf_op jit(solution)/shard_map/while/body/jit(dynamic_update_index_in_dim)/dynamic_update_slice | solution.py:128
  682.0 9.1 %dynamic_update_slice.23 = f32[4,2,5,4,16,128]{5,0,4,3,2,1:T(4,128)} dynamic-update-slice(f32[4,2,5,4,16,128]{5,0,4,3,2,1:T(4,128)} %get-tuple-element.1307, f32[1,2,5,4,16,128]{5,0,4,3,2,1:T(1,128)S(1)} %bitcast.272, s32[]{:T(128)S(6)} %sub.195, s32[]{:T(128)} %constant.243.clone.1..sunk.1, s32[]{:T(128)} %constant.243.clone.1..sunk.1, s32[]{:T(128)} %constant.243.clone.1..sunk.1, ...) | dynamic-update-slice | bytes 655364 | tf_op jit(solution)/shard_map/while/body/jit(dynamic_update_index_in_dim)/dynamic_update_slice | solution.py:128
  694.1 9.1 %dynamic_update_slice.23 = f32[4,2,5,4,16,128]{5,0,4,3,2,1:T(4,128)} dynamic-update-slice(f32[4,2,5,4,16,128]{5,0,4,3,2,1:T(4,128)} %get-tuple-element.1307, f32[1,2,5,4,16,128]{5,0,4,3,2,1:T(1,128)S(1)} %bitcast.272, s32[]{:T(128)S(6)} %sub.195, s32[]{:T(128)} %constant.243.clone.1..sunk.1, s32[]{:T(128)} %constant.243.clone.1..sunk.1, s32[]{:T(128)} %constant.243.clone.1..sunk.1, ...) | dynamic-update-slice | bytes 655364 | tf_op jit(solution)/shard_map/while/body/jit(dynamic_update_index_in_dim)/dynamic_update_slice | solution.py:128
  (516 shorter events, 175.5 us)
Async XLA Ops:
  6.5 100.1 %all-gather.10.cloned.1.call-start = ((), (), s32[]{:S(2)}) async-start(), calls=%async_computation | async-start | bytes 5898240 | tf_op jit(solution)/shard_map/all_gather | solution.py:109
  8.6 1.1 copy-start.10
  8.6 209.9 %all-gather.14.cloned.1.call-start = ((), (), s32[]{:S(2)}) async-start(), calls=%async_computation.2 | async-start | bytes 10813440 | tf_op jit(solution)/shard_map/all_gather | solution.py:13
  8.8 100.9 %copy-start = (f32[2,5,5,16,128]{4,3,2,1,0:T(8,128)}, f32[2,5,5,16,128]{4,3,2,1,0:T(8,128)S(1)}, u32[]{:S(2)}) copy-start(f32[2,5,5,16,128]{4,3,2,1,0:T(8,128)S(1)} %stack.192) | copy-start | bytes 1228804
  8.8 1.4 copy-start.11
  9.7 1.5 copy-start.12
  106.6 5.9 copy-start.5
  116.0 1.2 copy-start.4
  142.6 0.7 copy-start.8
  142.6 0.9 copy-start.3
  142.6 1.5 copy-start.9
  143.3 158.6 %all-gather.12.cloned.1.call-start = ((), (), s32[]{:S(2)}) async-start(), calls=%async_computation.1 | async-start | bytes 13516800 | tf_op jit(solution)/shard_map/all_gather | solution.py:13
  144.1 346.8 %all-gather.18.cloned.1.call-start = ((), (), s32[]{:S(2)}) async-start(), calls=%async_computation.4 | async-start | bytes 10813440 | tf_op jit(solution)/shard_map/all_gather | solution.py:13
  381.5 19.7 %copy-start.1 = (f32[2,5,5,16,128]{4,3,2,1,0:T(8,128)S(1)}, f32[2,5,5,16,128]{4,3,2,1,0:T(8,128)}, u32[]{:S(2)}) copy-start(f32[2,5,5,16,128]{4,3,2,1,0:T(8,128)} %copy-done) | copy-start | bytes 1228804
  385.0 1.3 copy-start.6
  389.9 1.3 copy-start.6
  394.8 1.3 copy-start.6
  399.7 1.3 copy-start.6
  414.6 0.7 copy-start.7
  414.6 0.8 copy-start.2
  415.4 158.7 %all-gather.16.cloned.1.call-start = ((), (), s32[]{:S(2)}) async-start(), calls=%async_computation.3 | async-start | bytes 13516800 | tf_op jit(solution)/shard_map/all_gather | solution.py:13
Sparse Core Ops, SparseCore 0:
  9.8 96.7 all-gather.9
  143.4 75.0 all-gather.13
  220.4 81.4 all-gather.11
  415.5 75.2 all-gather.17
  492.5 81.4 all-gather.15
where the time goes:
time: 715 us; the launch traced here: 710 us
  waiting for transfers between devices  409 us (57%)
  local copies, waits for them, and re-layouts  135 us (19%)
  other arithmetic  107 us (15%)
  loops' own time  34.9 us (5%)
  between operations  13.4 us (2%)
  matrix products  9.96 us (1%)
    all_gather x4, waiting for transfers between devices, entering(): everything = jax.tree.map(lambda part: lax.all_gather(part, axis), x)  315 us
    all_gather x1, waiting for transfers between devices, local(): lax.all_gather(forcing, 'span', axis=3, tiled=True).astype(jnp.float32)  93.4 us
    mul x176, local copies, waits for them, and re-layouts, small_product(): real = jnp.sum(left_re * right_re - left_im * right_im, axis=1)  70.8 us
    select_n x64, other arithmetic, lap(): return jax.tree.map(lambda a, b: jnp.where(reached, a, b), new, before)  69.7 us
    dynamic_update_slice x4, local copies, waits for them, and re-layouts, local(): lax.scan(local_forward, (vector_zero, identity), heights)  36.5 us
    reduce_sum x92, other arithmetic, small_product(): real = jnp.sum(left_re * right_re - left_im * right_im, axis=1)  21.5 us
  transfers between devices with their start and end apart: 5, of which 5 were waited for; matrix products, arithmetic and copies ran while one was open for 1% of the time, Pallas kernels for 0%

commit v1 on v0

v1 whole, which is shorter than its diff:
```python
import functools
import math

import jax
import jax.numpy as jnp
import numpy as np
from jax import lax
from jax.experimental import pallas as pl
from jax.experimental.pallas import tpu as pltpu
from jax.sharding import PartitionSpec as P

MESH = pl.DeviceIdType.MESH
F = 5
S = 8
K = 16
ROWS = 8
TR = 80
AR = 24
HI = lax.Precision.HIGHEST


def apply(coef, y, vectors):
    out = [None] * len(vectors)
    for j in range(F):
        cr = coef[y, 0, j]
        ci = coef[y, 1, j]
        for n, (vr, vi) in enumerate(vectors):
            xr = vr[j][None]
            xi = vi[j][None]
            re = cr * xr - ci * xi
            im = cr * xi + ci * xr
            out[n] = (re, im) if out[n] is None else (out[n][0] + re, out[n][1] + im)
    return out


def sub(a, b):
    return [(x[0] - y[0], x[1] - y[1]) for x, y in zip(a, b)]


def kernel(
    forcing, factor, table, piv, low, upp, out,
    tmp, send_f, recv_f, part_p, part_l, part_u, pf, lf, uf, pre, tm, a_hi, a_lo,
    send_r, driv, send_t, recv_t, te, send_a, recv_a, send_s, recv_s, src, sw, qb, resp,
    c_send, c_recv, f_send, f_recv, r_send, r_recv, t_send, t_recv, a_send, a_recv, s_send, s_recv,
    o_send, o_recv, loc,
):
    me_s = lax.axis_index("span")
    me_w = lax.axis_index("wall")
    core = lax.rem(me_w, 2)
    chip = me_w // 2
    other = 1 - core
    partner = chip * 2 + other

    def span_peer(o):
        return lax.rem(me_s + o, S)

    def wall_peer(o):
        return lax.rem(chip + o, K)

    barrier = pltpu.get_barrier_semaphore()

    def greet(s, w):
        pl.semaphore_signal(barrier, inc=1, device_id=(s, w), device_id_type=MESH)

    def greet_span(o, carry):
        greet(span_peer(o), me_w)
        greet(span_peer(o), partner)
        return carry

    def greet_wall(o, carry):
        greet(me_s, wall_peer(o) * 2 + core)
        return carry

    lax.fori_loop(1, S, greet_span, 0)
    lax.fori_loop(1, K, greet_wall, 0)
    greet(me_s, partner)

    def regroup(g, carry):
        for col in range(4):
            tmp[pl.ds(col * 64, 64), :] = forcing[g, col].astype(jnp.float32)
        for col in range(4):
            for y in range(4):
                piece = tmp[pl.ds(col * 64 + y, 16, stride=4), :].astype(jnp.bfloat16)
                send_f[col // 2, (col % 2) * 4 + y, lax.rem(g, F), g // F] = piece
        return carry

    lax.fori_loop(0, 2 * F, regroup, 0)

    pl.semaphore_wait(barrier, 2 * S - 1 + K - 1)

    def remote(src_ref, dst_ref, ss, rs, s, w):
        return pltpu.make_async_remote_copy(
            src_ref=src_ref, dst_ref=dst_ref, send_sem=ss, recv_sem=rs,
            device_id=(s, w), device_id_type=MESH,
        )

    def f_copy(ch, o):
        to = span_peer(o)
        return remote(send_f.at[ch, to], recv_f.at[ch, me_s], f_send.at[ch, to], f_recv.at[ch, me_s], to, me_w)

    def f_wait(ch, o):
        frm = span_peer(o)
        return remote(send_f.at[ch, frm], recv_f.at[ch, frm], f_send.at[ch, frm], f_recv.at[ch, frm], frm, me_w)

    def f_local(ch):
        return pltpu.make_async_copy(send_f.at[ch, me_s], recv_f.at[ch, me_s], loc.at[0, ch])

    def c_copy(n, ref, part):
        return remote(ref.at[:, pl.ds(other * 32, 32), :], part, c_send.at[n], c_recv.at[n], me_s, partner)

    c_copies = [c_copy(0, low, part_l), c_copy(1, upp, part_u), c_copy(2, piv, part_p)]
    for copy in c_copies:
        copy.start()
    for ch in range(2):
        f_local(ch).start()

        def start_f(o, carry):
            f_copy(ch, o).start()
            return carry

        lax.fori_loop(1, S, start_f, 0)

    def by_row(ref, first, dst, at):
        def step(g, carry):
            for j in range(F):
                tmp[pl.ds(j * 32, 32), :] = ref[g * F + j, pl.ds(first, 32), :].astype(jnp.float32)
            for j in range(F):
                for y in range(4):
                    dst[at * 4 + y, g // F, j, lax.rem(g, F)] = tmp[pl.ds(j * 32 + y, 8, stride=4), :]
            return carry

        lax.fori_loop(0, 2 * F, step, 0)

    mine = pl.multiple_of(core * 32, 32)
    by_row(low, mine, lf, core)
    by_row(upp, mine, uf, core)
    by_row(piv, mine, pf, core)
    c_copies[0].wait()
    by_row(part_l, 0, lf, other)
    c_copies[1].wait()
    by_row(part_u, 0, uf, other)
    c_copies[2].wait()
    by_row(part_p, 0, pf, other)

    def forward_column(n, carry):
        v = (-lf[0, 0, n], -lf[0, 1, n])
        pre[0, 0, n] = v[0]
        pre[0, 1, n] = v[1]

        def step(y, v):
            w = apply(lf, y, [v])[0]
            w = (-w[0], -w[1])
            pre[y, 0, n] = w[0]
            pre[y, 1, n] = w[1]
            return w

        v = lax.fori_loop(1, ROWS, step, v)
        tm[0, 0, n] = v[0]
        tm[0, 1, n] = v[1]
        return carry

    lax.fori_loop(0, F, forward_column, 0)

    def backward_column(n, carry):
        last = ROWS - 1
        v = (-uf[last, 0, n], -uf[last, 1, n])
        b = (pre[last, 0, n], pre[last, 1, n])

        def step(t, state):
            y = last - 1 - t
            v, b = state
            x, z = apply(uf, y, [v, b])
            return ((-x[0], -x[1]), (pre[y, 0, n] - z[0], pre[y, 1, n] - z[1]))

        v, b = lax.fori_loop(0, last, step, (v, b))
        tm[1, 0, n] = v[0]
        tm[1, 1, n] = v[1]
        tm[2, 0, n] = b[0]
        tm[2, 1, n] = b[1]
        return carry

    lax.fori_loop(0, F, backward_column, 0)

    def halves(p, q):
        axis = p.ndim - 1
        left = lax.broadcasted_iota(jnp.int32, p.shape, axis) < 64
        return (
            jnp.where(left, p, pltpu.roll(q, 64, axis)),
            jnp.where(left, pltpu.roll(p, 64, axis), q),
        )

    def pack_t(g, carry):
        d0, d1 = halves(tm[g // F, 0, lax.rem(g, F)], tm[g // F, 1, lax.rem(g, F)])
        for i in range(F):
            send_t[pl.ds(g * F + i, 8, stride=TR), :] = d0[i]
            send_t[pl.ds(8 * TR + g * F + i, 8, stride=TR), :] = d1[i]
        return carry

    lax.fori_loop(0, 3 * F, pack_t, 0)

    def t_block(k):
        return pl.ds(pl.multiple_of(k * TR, 8), TR)

    def t_copy(o):
        to = wall_peer(o)
        return remote(send_t.at[t_block(to)], recv_t.at[t_block(chip)], t_send.at[to], t_recv.at[chip], me_s, to * 2 + core)

    def t_wait(o):
        frm = wall_peer(o)
        return remote(send_t.at[t_block(frm)], recv_t.at[t_block(frm)], t_send.at[frm], t_recv.at[frm], me_s, frm * 2 + core)

    t_local = pltpu.make_async_copy(send_t.at[t_block(chip)], recv_t.at[t_block(chip)], loc.at[1, 0])
    t_local.start()

    def start_t(o, carry):
        t_copy(o).start()
        return carry

    lax.fori_loop(1, K, start_t, 0)

    def build(f, carry):
        fr = factor[f, 0:1, :]
        fi = factor[f, 1:2, :]
        cosine = table[0]
        sine = table[1]
        gr = cosine * fr - sine * fi
        gi = cosine * fi + sine * fr
        dot = functools.partial(jnp.dot, precision=HI, preferred_element_type=jnp.float32)
        kr = (dot(gr, cosine) + dot(gi, sine)) * (1.0 / 128.0)
        ki = (dot(gi, cosine) - dot(gr, sine)) * (1.0 / 128.0)
        for rows, cols, block in ((0, 0, kr), (0, 128, -ki), (128, 0, ki), (128, 128, kr)):
            top = block.astype(jnp.bfloat16)
            a_hi[f, rows:rows + 128, cols:cols + 128] = top
            a_lo[f, rows:rows + 128, cols:cols + 128] = (block - top.astype(jnp.float32)).astype(jnp.bfloat16)
        return carry

    lax.fori_loop(0, F, build, 0)

    def r_copy(ch, o, d):
        to = span_peer(o)
        c = core if d == 0 else other
        slot = core * S + me_s
        return remote(
            send_r.at[ch, to, c], driv.at[ch, slot], r_send.at[ch, c * S + to], r_recv.at[ch, slot], to, chip * 2 + c
        )

    def r_wait(ch, o, d):
        frm = span_peer(o)
        c = core if d == 0 else other
        slot = c * S + frm
        return remote(
            send_r.at[ch, frm, c], driv.at[ch, slot], r_send.at[ch, slot], r_recv.at[ch, slot], frm, chip * 2 + c
        )

    def r_local(ch):
        return pltpu.make_async_copy(send_r.at[ch, me_s, core], driv.at[ch, core * S + me_s], loc.at[2, ch])

    def filtered(ch, carry):
        f_local(ch).wait()

        def wait_f(o, carry):
            f_wait(ch, o).wait_recv()
            return carry

        lax.fori_loop(1, S, wait_f, 0)

        def field(f, carry):
            rhs = jnp.concatenate(
                [recv_f[ch, :, f, 0].reshape(128, 128), recv_f[ch, :, f, 1].reshape(128, 128)], axis=0
            )
            res = jnp.dot(a_hi[f], rhs, preferred_element_type=jnp.float32) + jnp.dot(
                a_lo[f], rhs, preferred_element_type=jnp.float32
            )
            send_r[ch, :, :, f, 0] = res[:128].reshape(S, 2, 8, 128)
            send_r[ch, :, :, f, 1] = res[128:].reshape(S, 2, 8, 128)
            return carry

        lax.fori_loop(0, F, field, 0)
        r_local(ch).start()
        r_copy(ch, 0, 1).start()

        def start_r(o, carry):
            r_copy(ch, o, 0).start()
            r_copy(ch, o, 1).start()
            return carry

        lax.fori_loop(1, S, start_r, 0)
        return carry

    lax.fori_loop(0, 2, filtered, 0)

    def a_block(ch, k):
        return pl.ds(pl.multiple_of((ch * K + k) * AR, 8), AR)

    def a_copy(ch, o):
        to = wall_peer(o)
        return remote(
            send_a.at[a_block(ch, to)], recv_a.at[a_block(ch, chip)], a_send.at[ch, to], a_recv.at[ch, chip], me_s, to * 2 + core
        )

    def a_wait(ch, o):
        frm = wall_peer(o)
        return remote(
            send_a.at[a_block(ch, frm)], recv_a.at[a_block(ch, frm)], a_send.at[ch, frm], a_recv.at[ch, frm], me_s, frm * 2 + core
        )

    def a_local(ch):
        return pltpu.make_async_copy(send_a.at[a_block(ch, chip)], recv_a.at[a_block(ch, chip)], loc.at[3, ch])

    zero = jnp.zeros((F, 8, 128), jnp.float32)

    def put(ref, y, state):
        for n in range(2):
            ref[y, n, 0] = state[n][0]
            ref[y, n, 1] = state[n][1]

    def get(ref, y):
        return [(ref[y, n, 0], ref[y, n, 1]) for n in range(2)]

    def local_solve(ch, carry):
        r_local(ch).wait()
        r_wait(ch, 0, 1).wait_recv()

        def wait_r(o, carry):
            r_wait(ch, o, 0).wait_recv()
            r_wait(ch, o, 1).wait_recv()
            return carry

        lax.fori_loop(1, S, wait_r, 0)

        def forward(y, state):
            base = (y // 4) * S + lax.rem(y, 4)
            drive = [(driv[ch, base + 4 * n, :, 0], driv[ch, base + 4 * n, :, 1]) for n in range(2)]
            source = apply(pf, y, drive)
            put(src.at[ch], y, source)
            state = sub(source, apply(lf, y, state))
            put(sw, y, state)
            return state

        a = lax.fori_loop(0, ROWS, forward, [(zero, zero), (zero, zero)])

        def backward(t, state):
            y = ROWS - 2 - t
            return sub(get(sw, y), apply(uf, y, state))

        c = lax.fori_loop(0, ROWS - 1, backward, a)
        base = ch * (K * AR)
        for g, (p, q) in enumerate(((a[0][0], a[1][0]), (a[0][1], a[1][1]), (c[0][0], c[1][0]), (c[0][1], c[1][1]))):
            d0, d1 = halves(p, q)
            for i in range(F):
                send_a[pl.ds(base + g * F + i, 8, stride=AR), :] = d0[i]
                send_a[pl.ds(base + 8 * AR + g * F + i, 8, stride=AR), :] = d1[i]
        a_local(ch).start()

        def start_a(o, carry):
            a_copy(ch, o).start()
            return carry

        lax.fori_loop(1, K, start_a, 0)
        return carry

    lax.fori_loop(0, 2, local_solve, 0)

    t_local.wait()

    def wait_t(o, carry):
        t_wait(o).wait_recv()
        return carry

    lax.fori_loop(1, K, wait_t, 0)

    def expand(k, carry):
        for g in range(3 * F):
            rows = recv_t[pl.ds(k * TR + g * F, F), :]
            left = lax.broadcasted_iota(jnp.int32, rows.shape, 1) < 64
            turned = pltpu.roll(rows, 64, 1)
            te[k, g // F, 0, g % F, 0:F, :] = jnp.where(left, rows, turned)
            te[k, g // F, 1, g % F, 0:F, :] = jnp.where(left, turned, rows)
        return carry

    lax.fori_loop(0, K, expand, 0)

    def small(k, m, state, start):
        re, im = start
        for j in range(F):
            tr = te[k, m, 0, j, 0:F, :]
            ti = te[k, m, 1, j, 0:F, :]
            xr = state[0][j:j + 1]
            xi = state[1][j:j + 1]
            re = re + (tr * xr - ti * xi)
            im = im + (tr * xi + ti * xr)
        return re, im

    def s_copy(ch, o):
        to = wall_peer(o)
        return remote(
            send_s.at[a_block(ch, to)], recv_s.at[a_block(ch, chip)], s_send.at[ch, to], s_recv.at[ch, chip], me_s, to * 2 + core
        )

    def s_wait(ch, o):
        frm = wall_peer(o)
        return remote(
            send_s.at[a_block(ch, frm)], recv_s.at[a_block(ch, frm)], s_send.at[ch, frm], s_recv.at[ch, frm], me_s, frm * 2 + core
        )

    def s_local(ch):
        return pltpu.make_async_copy(send_s.at[a_block(ch, chip)], recv_s.at[a_block(ch, chip)], loc.at[4, ch])

    flat = jnp.zeros((F, 128), jnp.float32)

    def owner_scan(ch, carry):
        a_local(ch).wait()

        def wait_a(o, carry):
            a_wait(ch, o).wait_recv()
            return carry

        lax.fori_loop(1, K, wait_a, 0)

        def forward(k, state):
            base = (ch * K + k) * AR
            send_s[pl.ds(base, F), :] = state[0]
            send_s[pl.ds(base + F, F), :] = state[1]
            a = (recv_a[pl.ds(base, F), :], recv_a[pl.ds(base + F, F), :])
            c = (recv_a[pl.ds(base + 2 * F, F), :], recv_a[pl.ds(base + 3 * F, F), :])
            q = small(k, 2, state, c)
            qb[k, 0, 0:F, :] = q[0]
            qb[k, 1, 0:F, :] = q[1]
            return small(k, 0, state, a)

        lax.fori_loop(0, K, forward, (flat, flat))

        def backward(t, state):
            k = K - 1 - t
            base = (ch * K + k) * AR
            send_s[pl.ds(base + 2 * F, F), :] = state[0]
            send_s[pl.ds(base + 3 * F, F), :] = state[1]
            return small(k, 1, state, (qb[k, 0, 0:F, :], qb[k, 1, 0:F, :]))

        lax.fori_loop(0, K, backward, (flat, flat))
        s_local(ch).start()

        def start_s(o, carry):
            s_copy(ch, o).start()
            return carry

        lax.fori_loop(1, K, start_s, 0)
        return carry

    lax.fori_loop(0, 2, owner_scan, 0)

    def o_copy(ch):
        return remote(
            resp.at[other, ch], out.at[:, pl.ds(2 * ch, 2), pl.ds(core * 32, 32), :],
            o_send.at[ch], o_recv.at[ch], me_s, partner,
        )

    def o_wait(ch):
        return remote(
            resp.at[other, ch], out.at[:, pl.ds(2 * ch, 2), pl.ds(other * 32, 32), :],
            o_send.at[ch], o_recv.at[ch], me_s, partner,
        )

    def o_local(ch):
        return pltpu.make_async_copy(
            resp.at[core, ch], out.at[:, pl.ds(2 * ch, 2), pl.ds(core * 32, 32), :], loc.at[5, ch]
        )

    def final(ch, carry):
        s_local(ch).wait()

        def wait_s(o, carry):
            s_wait(ch, o).wait_recv()
            return carry

        lax.fori_loop(1, K, wait_s, 0)
        base = ch * (K * AR)

        def entering(g):
            e0 = jnp.stack([recv_s[pl.ds(base + g * F + i, 8, stride=AR), :] for i in range(F)])
            e1 = jnp.stack([recv_s[pl.ds(base + 8 * AR + g * F + i, 8, stride=AR), :] for i in range(F)])
            return halves(e0, e1)

        def pair(g):
            re = entering(g)
            im = entering(g + 1)
            return [(re[0], im[0]), (re[1], im[1])]

        def forward(y, state):
            state = sub(get(src.at[ch], y), apply(lf, y, state))
            put(sw, y, state)
            return state

        lax.fori_loop(0, ROWS, forward, pair(0))

        def backward(t, state):
            y = ROWS - 1 - t
            state = sub(get(sw, y), apply(uf, y, state))
            for n in range(2):
                for ri in range(2):
                    for i in range(F):
                        resp.at[y // 4, ch, ri * F + i, n][pl.ds(lax.rem(y, 4), 8, stride=4), :] = state[n][ri][i]
            return state

        lax.fori_loop(0, ROWS, backward, pair(2))
        o_local(ch).start()
        o_copy(ch).start()
        return carry

    lax.fori_loop(0, 2, final, 0)

    for ch in range(2):
        o_local(ch).wait()
        o_wait(ch).wait_recv()
        o_copy(ch).wait_send()
        r_copy(ch, 0, 1).wait_send()

        def end_span(o, carry):
            f_copy(ch, o).wait_send()
            r_copy(ch, o, 0).wait_send()
            r_copy(ch, o, 1).wait_send()
            return carry

        def end_wall(o, carry):
            a_copy(ch, o).wait_send()
            s_copy(ch, o).wait_send()
            return carry

        lax.fori_loop(1, S, end_span, 0)
        lax.fori_loop(1, K, end_wall, 0)

    def end_t(o, carry):
        t_copy(o).wait_send()
        return carry

    lax.fori_loop(1, K, end_t, 0)


def tables():
    n = np.arange(128)
    angle = (n[:, None] * n[None, :] % 128) * (2.0 * math.pi / 128)
    return np.stack([np.cos(angle), np.sin(angle)]).astype(np.float32)


def local(forcing, span_factor, pivot_inverse, step_lower, step_upper):
    f32, bf16 = jnp.float32, jnp.bfloat16
    dma = pltpu.SemaphoreType.DMA
    vm = pltpu.VMEM
    flat = [x.reshape(50, 64, 128) for x in (pivot_inverse, step_lower, step_upper)]
    coef = vm((ROWS, 2, F, F, 8, 128), f32)
    rows = vm((ROWS, 2, 2, F, 8, 128), f32)
    scratch = [
        vm((256, 128), f32),
        vm((2, S, F, 2, 16, 128), bf16),
        vm((2, S, F, 2, 16, 128), bf16),
        vm((50, 32, 128), bf16), vm((50, 32, 128), bf16), vm((50, 32, 128), bf16),
        coef, coef, coef, coef,
        vm((3, 2, F, F, 8, 128), f32),
        vm((F, 256, 256), bf16), vm((F, 256, 256), bf16),
        vm((2, S, 2, F, 2, 8, 128), f32),
        vm((2, 2 * S, F, 2, 8, 128), f32),
        vm((K * TR, 128), f32), vm((K * TR, 128), f32),
        vm((K, 3, 2, F, 8, 128), f32),
        vm((2 * K * AR, 128), f32), vm((2 * K * AR, 128), f32),
        vm((2 * K * AR, 128), f32), vm((2 * K * AR, 128), f32),
        vm((2, ROWS, 2, 2, F, 8, 128), f32),
        rows,
        vm((K, 2, 8, 128), f32),
        vm((2, 2, 2 * F, 2, 32, 128), f32),
        dma((3,)), dma((3,)),
        dma((2, S)), dma((2, S)),
        dma((2, 2 * S)), dma((2, 2 * S)),
        dma((K,)), dma((K,)),
        dma((2, K)), dma((2, K)),
        dma((2, K)), dma((2, K)),
        dma((2,)), dma((2,)),
        dma((6, 2)),
    ]
    out = pl.pallas_call(
        kernel,
        out_shape=jax.ShapeDtypeStruct((2 * F, 4, 64, 128), f32),
        in_specs=[pl.BlockSpec(memory_space=pltpu.VMEM)] * 6,
        out_specs=pl.BlockSpec(memory_space=pltpu.VMEM),
        scratch_shapes=scratch,
        compiler_params=pltpu.CompilerParams(
            collective_id=0, has_side_effects=True, vmem_limit_bytes=56 << 20
        ),
    )(
        forcing.reshape(2 * F, 4, 64, 128),
        jnp.swapaxes(span_factor, 0, 1),
        jnp.asarray(tables()),
        *flat,
    )
    return out.reshape(2, F, 4, 16, 4, 128)


def solution(mesh):
    placed = P(None, None, None, "span", "wall", None)
    return jax.shard_map(
        local,
        mesh=mesh,
        in_specs=(placed, P(), placed, placed, placed),
        out_specs=placed,
        check_vma=False,
    )
```

time: 715 us -> 75.7 us (0.11)
  waiting for transfers between devices: 409 us -> 0 us
  local copies, waits for them, and re-layouts: 135 us -> 2.52 us
  other arithmetic: 107 us -> 0 us
  Pallas kernels: 0 us -> 73.1 us
  loops' own time: 34.9 us -> 0 us
  between operations: 13.4 us -> 0.01 us
  matrix products: 9.96 us -> 0 us
    all_gather x5 -> x0, waiting for transfers between devices: 408 us -> none  [the longest x4 315 us: entering(): everything = jax.tree.map(lambda part: lax.all_gather(part, axis), x)]
    pallas_call x0 -> x1, Pallas kernels: none -> 73.1 us  [local(): pl.pallas_call(kernel, out_shape=jax.ShapeDtypeStruct((2 * F, 4, 64, 128)...]
    mul x177 -> x0, local copies, waits for them, and re-layouts: 70.8 us -> none  [the longest x176 70.8 us: small_product(): real = jnp.sum(left_re * right_re - left_im * right_im, axis=1)]
    select_n x64 -> x0, other arithmetic: 69.7 us -> none  [lap(): return jax.tree.map(lambda a, b: jnp.where(reached, a, b), new, before)]
    dynamic_update_slice x4 -> x0, local copies, waits for them, and re-layouts: 36.5 us -> none  [local(): lax.scan(local_forward, (vector_zero, identity), heights)]
    another operation x6 -> x0, loops' own time: 34.9 us -> none  [the longest x1 8.1 us: local(): lax.scan(local_backward, (vector_zero, identity), (heights, sweeps), reve...]
    reduce_sum x92 -> x0, other arithmetic: 21.5 us -> none  [small_product(): real = jnp.sum(left_re * right_re - left_im * right_im, axis=1)]
    dynamic_slice x20 -> x0, local copies, waits for them, and re-layouts: 13.7 us -> none  [the longest x16 9.7 us: local(): lax.scan(local_forward, (vector_zero, identity), heights)]
  transfers between devices with their start and end apart: 5 -> 0, of which waited for: 5 -> 0; matrix products, arithmetic and copies ran while one was open for 1% -> 0% of each run, Pallas kernels for 0% -> 0%
where the time goes in v1:
time: 75.7 us; the launch traced here: 75.6 us
  Pallas kernels  73.1 us (97%)
  local copies, waits for them, and re-layouts  2.52 us (3%)
    pallas_call x1, Pallas kernels, local(): pl.pallas_call(kernel, out_shape=jax.ShapeDtypeStruct((2 * F, 4, 64, 128)...  73.1 us
    unnamed x1, local copies, waits for them, and re-layouts  2.52 us

profile of v1, /device:TPU:1, one launch (start us, length us, event | category | flops | bytes accessed | tf_op | source)
XLA Modules:
  0.0 75.6 jit_solution(14123562258025238172)
XLA Ops:
  0.0 73.1 %shard_map.64 = f32[10,4,64,128]{3,2,1,0:T(8,128)} custom-call(bf16[10,4,64,128]{3,2,1,0:T(8,128)(2,1)} %bitcast.10, f32[5,2,128]{2,1,0:T(2,128)} %bitcast.11, f32[2,128,128]{2,1,0:T(8,128)} %constant.2.clone.table, bf16[50,64,128]{2,1,0:T(8,128)(2,1)} %bitcast.7, bf16[50,64,128]{2,1,0:T(8,128)(2,1)} %bitcast.8, bf16[50,64,128]{2,1,0:T(8,128)(2,1)} %bitcast.9), custom_call_target="tpu_custom_call" | custom-call | tf_op jit(solution)/shard_map/pallas_call | solution.py:579
  73.1 2.5 %copy.8 = f32[2,5,4,16,4,128]{5,4,3,2,1,0:T(4,128)} copy(f32[2,5,4,16,4,128]{5,4,3,2,1,0:T(4,128)} %bitcast.6) | data formatting | bytes 2621440

commit v2 on v1

--- a/solution.py
+++ b/solution.py
@@ -17,6 +17,23 @@
 TR = 80
 AR = 24
 HI = lax.Precision.HIGHEST
+LEVELS = 29900.0
+SHIFT = 117.0
+
+
+def encode(x, scale):
+    y = x * (LEVELS / scale)
+    n = jnp.floor(jnp.abs(y) + 0.5)
+    e = jnp.floor(n * (1.0 / 128.0))
+    v = (1.0 + (n - 128.0 * e) * (1.0 / 128.0)) * jnp.exp2(e - SHIFT)
+    return jnp.where(y < 0.0, -v, v)
+
+
+def decode(v, scale):
+    a = jnp.abs(v)
+    e = jnp.floor(jnp.log2(a) + 0.002)
+    n = 128.0 * (e + (SHIFT - 1.0)) + 128.0 * (a * jnp.exp2(-e))
+    return jnp.where(v < 0.0, -n, n) * (scale * (1.0 / LEVELS))
 
 
 def apply(coef, y, vectors):
@@ -38,11 +55,11 @@
 
 
 def kernel(
-    forcing, factor, table, piv, low, upp, out,
-    tmp, send_f, recv_f, part_p, part_l, part_u, pf, lf, uf, pre, tm, a_hi, a_lo,
+    forcing_in, factor_in, table_in, piv_in, low_in, upp_in, out,
+    forcing, factor, table, piv, low, upp, tmp, scales, send_f, recv_f, part_p, part_l, part_u, pf, lf, uf, pre, tm, a_hi, a_lo,
     send_r, driv, send_t, recv_t, te, send_a, recv_a, send_s, recv_s, src, sw, qb, resp,
     c_send, c_recv, f_send, f_recv, r_send, r_recv, t_send, t_recv, a_send, a_recv, s_send, s_recv,
-    o_send, o_recv, loc,
+    o_send, o_recv, loc, load,
 ):
     me_s = lax.axis_index("span")
     me_w = lax.axis_index("wall")
@@ -57,6 +74,18 @@
     def wall_peer(o):
         return lax.rem(chip + o, K)
 
+    loads = [
+        pltpu.make_async_copy(a, b, load.at[n])
+        for n, (a, b) in enumerate(
+            (
+                (forcing_in, forcing), (low_in, low), (upp_in, upp), (piv_in, piv),
+                (factor_in, factor), (table_in, table),
+            )
+        )
+    ]
+    for copy in loads:
+        copy.start()
+
     barrier = pltpu.get_barrier_semaphore()
 
     def greet(s, w):
@@ -84,7 +113,10 @@
                 send_f[col // 2, (col % 2) * 4 + y, lax.rem(g, F), g // F] = piece
         return carry
 
+    loads[0].wait()
     lax.fori_loop(0, 2 * F, regroup, 0)
+    for copy in loads[1:]:
+        copy.wait()
 
     pl.semaphore_wait(barrier, 2 * S - 1 + K - 1)
 
@@ -135,89 +167,6 @@
     by_row(low, mine, lf, core)
     by_row(upp, mine, uf, core)
     by_row(piv, mine, pf, core)
-    c_copies[0].wait()
-    by_row(part_l, 0, lf, other)
-    c_copies[1].wait()
-    by_row(part_u, 0, uf, other)
-    c_copies[2].wait()
-    by_row(part_p, 0, pf, other)
-
-    def forward_column(n, carry):
-        v = (-lf[0, 0, n], -lf[0, 1, n])
-        pre[0, 0, n] = v[0]
-        pre[0, 1, n] = v[1]
-
-        def step(y, v):
-            w = apply(lf, y, [v])[0]
-            w = (-w[0], -w[1])
-            pre[y, 0, n] = w[0]
-            pre[y, 1, n] = w[1]
-            return w
-
-        v = lax.fori_loop(1, ROWS, step, v)
-        tm[0, 0, n] = v[0]
-        tm[0, 1, n] = v[1]
-        return carry
-
-    lax.fori_loop(0, F, forward_column, 0)
-
-    def backward_column(n, carry):
-        last = ROWS - 1
-        v = (-uf[last, 0, n], -uf[last, 1, n])
-        b = (pre[last, 0, n], pre[last, 1, n])
-
-        def step(t, state):
-            y = last - 1 - t
-            v, b = state
-            x, z = apply(uf, y, [v, b])
-            return ((-x[0], -x[1]), (pre[y, 0, n] - z[0], pre[y, 1, n] - z[1]))
-
-        v, b = lax.fori_loop(0, last, step, (v, b))
-        tm[1, 0, n] = v[0]
-        tm[1, 1, n] = v[1]
-        tm[2, 0, n] = b[0]
-        tm[2, 1, n] = b[1]
-        return carry
-
-    lax.fori_loop(0, F, backward_column, 0)
-
-    def halves(p, q):
-        axis = p.ndim - 1
-        left = lax.broadcasted_iota(jnp.int32, p.shape, axis) < 64
-        return (
-            jnp.where(left, p, pltpu.roll(q, 64, axis)),
-            jnp.where(left, pltpu.roll(p, 64, axis), q),
-        )
-
-    def pack_t(g, carry):
-        d0, d1 = halves(tm[g // F, 0, lax.rem(g, F)], tm[g // F, 1, lax.rem(g, F)])
-        for i in range(F):
-            send_t[pl.ds(g * F + i, 8, stride=TR), :] = d0[i]
-            send_t[pl.ds(8 * TR + g * F + i, 8, stride=TR), :] = d1[i]
-        return carry
-
-    lax.fori_loop(0, 3 * F, pack_t, 0)
-
-    def t_block(k):
-        return pl.ds(pl.multiple_of(k * TR, 8), TR)
-
-    def t_copy(o):
-        to = wall_peer(o)
-        return remote(send_t.at[t_block(to)], recv_t.at[t_block(chip)], t_send.at[to], t_recv.at[chip], me_s, to * 2 + core)
-
-    def t_wait(o):
-        frm = wall_peer(o)
-        return remote(send_t.at[t_block(frm)], recv_t.at[t_block(frm)], t_send.at[frm], t_recv.at[frm], me_s, frm * 2 + core)
-
-    t_local = pltpu.make_async_copy(send_t.at[t_block(chip)], recv_t.at[t_block(chip)], loc.at[1, 0])
-    t_local.start()
-
-    def start_t(o, carry):
-        t_copy(o).start()
-        return carry
-
-    lax.fori_loop(1, K, start_t, 0)
-
     def build(f, carry):
         fr = factor[f, 0:1, :]
         fi = factor[f, 1:2, :]
@@ -236,6 +185,89 @@
 
     lax.fori_loop(0, F, build, 0)
 
+    c_copies[0].wait()
+    by_row(part_l, 0, lf, other)
+    c_copies[1].wait()
+    by_row(part_u, 0, uf, other)
+    c_copies[2].wait()
+    by_row(part_p, 0, pf, other)
+
+    def forward_column(n, carry):
+        v = (-lf[0, 0, n], -lf[0, 1, n])
+        pre[0, 0, n] = v[0]
+        pre[0, 1, n] = v[1]
+
+        def step(y, v):
+            w = apply(lf, y, [v])[0]
+            w = (-w[0], -w[1])
+            pre[y, 0, n] = w[0]
+            pre[y, 1, n] = w[1]
+            return w
+
+        v = lax.fori_loop(1, ROWS, step, v)
+        tm[0, 0, n] = v[0]
+        tm[0, 1, n] = v[1]
+        return carry
+
+    lax.fori_loop(0, F, forward_column, 0)
+
+    def backward_column(n, carry):
+        last = ROWS - 1
+        v = (-uf[last, 0, n], -uf[last, 1, n])
+        b = (pre[last, 0, n], pre[last, 1, n])
+
+        def step(t, state):
+            y = last - 1 - t
+            v, b = state
+            x, z = apply(uf, y, [v, b])
+            return ((-x[0], -x[1]), (pre[y, 0, n] - z[0], pre[y, 1, n] - z[1]))
+
+        v, b = lax.fori_loop(0, last, step, (v, b))
+        tm[1, 0, n] = v[0]
+        tm[1, 1, n] = v[1]
+        tm[2, 0, n] = b[0]
+        tm[2, 1, n] = b[1]
+        return carry
+
+    lax.fori_loop(0, F, backward_column, 0)
+
+    def halves(p, q):
+        axis = p.ndim - 1
+        left = lax.broadcasted_iota(jnp.int32, p.shape, axis) < 64
+        return (
+            jnp.where(left, p, pltpu.roll(q, 64, axis)),
+            jnp.where(left, pltpu.roll(p, 64, axis), q),
+        )
+
+    def pack_t(g, carry):
+        d0, d1 = halves(tm[g // F, 0, lax.rem(g, F)], tm[g // F, 1, lax.rem(g, F)])
+        for i in range(F):
+            send_t[pl.ds(g * F + i, 8, stride=TR), :] = d0[i]
+            send_t[pl.ds(8 * TR + g * F + i, 8, stride=TR), :] = d1[i]
+        return carry
+
+    lax.fori_loop(0, 3 * F, pack_t, 0)
+
+    def t_block(k):
+        return pl.ds(pl.multiple_of(k * TR, 8), TR)
+
+    def t_copy(o):
+        to = wall_peer(o)
+        return remote(send_t.at[t_block(to)], recv_t.at[t_block(chip)], t_send.at[to], t_recv.at[chip], me_s, to * 2 + core)
+
+    def t_wait(o):
+        frm = wall_peer(o)
+        return remote(send_t.at[t_block(frm)], recv_t.at[t_block(frm)], t_send.at[frm], t_recv.at[frm], me_s, frm * 2 + core)
+
+    t_local = pltpu.make_async_copy(send_t.at[t_block(chip)], recv_t.at[t_block(chip)], loc.at[1, 0])
+    t_local.start()
+
+    def start_t(o, carry):
+        t_copy(o).start()
+        return carry
+
+    lax.fori_loop(1, K, start_t, 0)
+
     def r_copy(ch, o, d):
         to = span_peer(o)
         c = core if d == 0 else other
@@ -271,11 +303,17 @@
             res = jnp.dot(a_hi[f], rhs, preferred_element_type=jnp.float32) + jnp.dot(
                 a_lo[f], rhs, preferred_element_type=jnp.float32
             )
-            send_r[ch, :, :, f, 0] = res[:128].reshape(S, 2, 8, 128)
-            send_r[ch, :, :, f, 1] = res[128:].reshape(S, 2, 8, 128)
+            re = res[:128].reshape(S, 2, 8, 128)
+            im = res[128:].reshape(S, 2, 8, 128)
+            top = jnp.max(jnp.maximum(jnp.abs(re), jnp.abs(im)), axis=2, keepdims=True)
+            scale = jnp.maximum(top * 1.01, 1e-30).astype(jnp.bfloat16).astype(jnp.float32)
+            scales[:, :, pl.ds(f, 1), :] = scale
+            codes = jnp.concatenate([encode(re, scale), encode(im, scale)], axis=2)
+            send_r[ch, :, :, f] = codes.astype(jnp.bfloat16)
             return carry
 
         lax.fori_loop(0, F, field, 0)
+        send_r[ch, :, :, F] = jnp.concatenate([scales[...], scales[...]], axis=2).astype(jnp.bfloat16)
         r_local(ch).start()
         r_copy(ch, 0, 1).start()
 
@@ -330,7 +368,13 @@
 
         def forward(y, state):
             base = (y // 4) * S + lax.rem(y, 4)
-            drive = [(driv[ch, base + 4 * n, :, 0], driv[ch, base + 4 * n, :, 1]) for n in range(2)]
+            drive = []
+            for n in range(2):
+                scale = driv[ch, base + 4 * n, F].astype(jnp.float32)
+                parts = [
+                    decode(driv[ch, base + 4 * n, f].astype(jnp.float32), scale[f:f + 1]) for f in range(F)
+                ]
+                drive.append((jnp.stack([x[:8] for x in parts]), jnp.stack([x[8:] for x in parts])))
             source = apply(pf, y, drive)
             put(src.at[ch], y, source)
             state = sub(source, apply(lf, y, state))
@@ -550,15 +594,18 @@
     coef = vm((ROWS, 2, F, F, 8, 128), f32)
     rows = vm((ROWS, 2, 2, F, 8, 128), f32)
     scratch = [
+        vm((2 * F, 4, 64, 128), bf16), vm((F, 2, 128), f32), vm((2, 128, 128), f32),
+        vm((50, 64, 128), bf16), vm((50, 64, 128), bf16), vm((50, 64, 128), bf16),
         vm((256, 128), f32),
+        vm((S, 2, 8, 128), f32),
         vm((2, S, F, 2, 16, 128), bf16),
         vm((2, S, F, 2, 16, 128), bf16),
         vm((50, 32, 128), bf16), vm((50, 32, 128), bf16), vm((50, 32, 128), bf16),
         coef, coef, coef, coef,
         vm((3, 2, F, F, 8, 128), f32),
         vm((F, 256, 256), bf16), vm((F, 256, 256), bf16),
-        vm((2, S, 2, F, 2, 8, 128), f32),
-        vm((2, 2 * S, F, 2, 8, 128), f32),
+        vm((2, S, 2, F + 1, 16, 128), bf16),
+        vm((2, 2 * S, F + 1, 16, 128), bf16),
         vm((K * TR, 128), f32), vm((K * TR, 128), f32),
         vm((K, 3, 2, F, 8, 128), f32),
         vm((2 * K * AR, 128), f32), vm((2 * K * AR, 128), f32),
@@ -575,12 +622,13 @@
         dma((2, K)), dma((2, K)),
         dma((2,)), dma((2,)),
         dma((6, 2)),
+        dma((6,)),
     ]
     out = pl.pallas_call(
         kernel,
         out_shape=jax.ShapeDtypeStruct((2 * F, 4, 64, 128), f32),
-        in_specs=[pl.BlockSpec(memory_space=pltpu.VMEM)] * 6,
-        out_specs=pl.BlockSpec(memory_space=pltpu.VMEM),
+        in_specs=[pl.BlockSpec(memory_space=pl.ANY)] * 6,
+        out_specs=pl.BlockSpec(memory_space=pl.ANY),
         scratch_shapes=scratch,
         compiler_params=pltpu.CompilerParams(
             collective_id=0, has_side_effects=True, vmem_limit_bytes=56 << 20

time: 75.7 us -> 67.4 us (0.89)
  Pallas kernels: 73.1 us -> 64.4 us
    pallas_call x1, Pallas kernels: 73.1 us -> 64.4 us  [local(): pl.pallas_call(kernel, out_shape=jax.ShapeDtypeStruct((2 * F, 4, 64, 128)...]
where the time goes in v2:
time: 67.4 us; the launch traced here: 67 us
  Pallas kernels  64.4 us (96%)
  local copies, waits for them, and re-layouts  2.52 us (4%)
    pallas_call x1, Pallas kernels, local(): pl.pallas_call(kernel, out_shape=jax.ShapeDtypeStruct((2 * F, 4, 64, 128)...  64.4 us
    unnamed x1, local copies, waits for them, and re-layouts  2.52 us

profile of v2, /device:TPU:1, one launch (start us, length us, event | category | flops | bytes accessed | tf_op | source)
XLA Modules:
  0.0 67.0 jit_solution(11461614138153857369)
XLA Ops:
  0.0 64.4 %shard_map.64 = f32[10,4,64,128]{3,2,1,0:T(8,128)} custom-call(bf16[10,4,64,128]{3,2,1,0:T(8,128)(2,1)} %bitcast.10, f32[5,2,128]{2,1,0:T(2,128)} %bitcast.11, f32[2,128,128]{2,1,0:T(8,128)} %constant.2.clone.table_in, bf16[50,64,128]{2,1,0:T(8,128)(2,1)} %bitcast.7, bf16[50,64,128]{2,1,0:T(8,128)(2,1)} %bitcast.8, bf16[50,64,128]{2,1,0:T(8,128)(2,1)} %bitcast.9), custom_call_target="tpu_custom_call" | custom-call | tf_op jit(solution)/shard_map/pallas_call | solution.py:627
  64.5 2.5 %copy.8 = f32[2,5,4,16,4,128]{5,4,3,2,1,0:T(4,128)} copy(f32[2,5,4,16,4,128]{5,4,3,2,1,0:T(4,128)} %bitcast.6) | data formatting | bytes 2621440

commit v3 on v2

--- a/solution.py
+++ b/solution.py
@@ -14,7 +14,7 @@
 S = 8
 K = 16
 ROWS = 8
-TR = 80
+TR = 96
 AR = 24
 HI = lax.Precision.HIGHEST
 LEVELS = 29900.0
@@ -34,6 +34,25 @@
     e = jnp.floor(jnp.log2(a) + 0.002)
     n = 128.0 * (e + (SHIFT - 1.0)) + 128.0 * (a * jnp.exp2(-e))
     return jnp.where(v < 0.0, -n, n) * (scale * (1.0 / LEVELS))
+
+
+def encode_blocks(src, dst, first, count, parts, tiles, used):
+    rows = parts * tiles * 8
+    x = src[pl.ds(pl.multiple_of(first * rows, 8), count * rows), :].reshape(count * parts, tiles, 8, 128)
+    place = lax.broadcasted_iota(jnp.int32, x.shape, 1) * 8 + lax.broadcasted_iota(jnp.int32, x.shape, 2)
+    good = place < used
+    x = jnp.where(good, x, 0.0)
+    top = jnp.max(jnp.max(jnp.abs(x), axis=1, keepdims=True), axis=2, keepdims=True)
+    scale = jnp.maximum(top * 1.01, 1e-30).astype(jnp.bfloat16).astype(jnp.float32)
+    code = jnp.where(good, encode(x, scale), scale).astype(jnp.bfloat16)
+    dst[pl.ds(first, count)] = code.reshape(count, parts * tiles, 8, 128)
+
+
+def decode_blocks(src, dst, first, count, parts, tiles):
+    rows = parts * tiles * 8
+    code = src[pl.ds(first, count)].astype(jnp.float32).reshape(count * parts, tiles, 8, 128)
+    x = decode(code, code[:, tiles - 1:, 7:, :])
+    dst[pl.ds(pl.multiple_of(first * rows, 8), count * rows), :] = x.reshape(count * rows, 128)
 
 
 def apply(coef, y, vectors):
@@ -57,7 +76,8 @@
 def kernel(
     forcing_in, factor_in, table_in, piv_in, low_in, upp_in, out,
     forcing, factor, table, piv, low, upp, tmp, scales, send_f, recv_f, part_p, part_l, part_u, pf, lf, uf, pre, tm, a_hi, a_lo,
-    send_r, driv, send_t, recv_t, te, send_a, recv_a, send_s, recv_s, src, sw, qb, resp,
+    send_r, driv, send_t, recv_t, te, send_a, recv_a, send_s, recv_s,
+    code_t, got_t, code_a, got_a, code_s, got_s, src, sw, qb, resp,
     c_send, c_recv, f_send, f_recv, r_send, r_recv, t_send, t_recv, a_send, a_recv, s_send, s_recv,
     o_send, o_recv, loc, load,
 ):
@@ -143,7 +163,8 @@
     c_copies = [c_copy(0, low, part_l), c_copy(1, upp, part_u), c_copy(2, piv, part_p)]
     for copy in c_copies:
         copy.start()
-    for ch in range(2):
+
+    def forcing_out(ch):
         f_local(ch).start()
 
         def start_f(o, carry):
@@ -151,6 +172,8 @@
             return carry
 
         lax.fori_loop(1, S, start_f, 0)
+
+    forcing_out(0)
 
     def by_row(ref, first, dst, at):
         def step(g, carry):
@@ -185,6 +208,7 @@
 
     lax.fori_loop(0, F, build, 0)
 
+    forcing_out(1)
     c_copies[0].wait()
     by_row(part_l, 0, lf, other)
     c_copies[1].wait()
@@ -210,63 +234,6 @@
         return carry
 
     lax.fori_loop(0, F, forward_column, 0)
-
-    def backward_column(n, carry):
-        last = ROWS - 1
-        v = (-uf[last, 0, n], -uf[last, 1, n])
-        b = (pre[last, 0, n], pre[last, 1, n])
-
-        def step(t, state):
-            y = last - 1 - t
-            v, b = state
-            x, z = apply(uf, y, [v, b])
-            return ((-x[0], -x[1]), (pre[y, 0, n] - z[0], pre[y, 1, n] - z[1]))
-
-        v, b = lax.fori_loop(0, last, step, (v, b))
-        tm[1, 0, n] = v[0]
-        tm[1, 1, n] = v[1]
-        tm[2, 0, n] = b[0]
-        tm[2, 1, n] = b[1]
-        return carry
-
-    lax.fori_loop(0, F, backward_column, 0)
-
-    def halves(p, q):
-        axis = p.ndim - 1
-        left = lax.broadcasted_iota(jnp.int32, p.shape, axis) < 64
-        return (
-            jnp.where(left, p, pltpu.roll(q, 64, axis)),
-            jnp.where(left, pltpu.roll(p, 64, axis), q),
-        )
-
-    def pack_t(g, carry):
-        d0, d1 = halves(tm[g // F, 0, lax.rem(g, F)], tm[g // F, 1, lax.rem(g, F)])
-        for i in range(F):
-            send_t[pl.ds(g * F + i, 8, stride=TR), :] = d0[i]
-            send_t[pl.ds(8 * TR + g * F + i, 8, stride=TR), :] = d1[i]
-        return carry
-
-    lax.fori_loop(0, 3 * F, pack_t, 0)
-
-    def t_block(k):
-        return pl.ds(pl.multiple_of(k * TR, 8), TR)
-
-    def t_copy(o):
-        to = wall_peer(o)
-        return remote(send_t.at[t_block(to)], recv_t.at[t_block(chip)], t_send.at[to], t_recv.at[chip], me_s, to * 2 + core)
-
-    def t_wait(o):
-        frm = wall_peer(o)
-        return remote(send_t.at[t_block(frm)], recv_t.at[t_block(frm)], t_send.at[frm], t_recv.at[frm], me_s, frm * 2 + core)
-
-    t_local = pltpu.make_async_copy(send_t.at[t_block(chip)], recv_t.at[t_block(chip)], loc.at[1, 0])
-    t_local.start()
-
-    def start_t(o, carry):
-        t_copy(o).start()
-        return carry
-
-    lax.fori_loop(1, K, start_t, 0)
 
     def r_copy(ch, o, d):
         to = span_peer(o)
@@ -325,25 +292,85 @@
         lax.fori_loop(1, S, start_r, 0)
         return carry
 
-    lax.fori_loop(0, 2, filtered, 0)
-
-    def a_block(ch, k):
-        return pl.ds(pl.multiple_of((ch * K + k) * AR, 8), AR)
+    filtered(0, 0)
+
+    def backward_column(n, carry):
+        last = ROWS - 1
+        v = (-uf[last, 0, n], -uf[last, 1, n])
+        b = (pre[last, 0, n], pre[last, 1, n])
+
+        def step(t, state):
+            y = last - 1 - t
+            v, b = state
+            x, z = apply(uf, y, [v, b])
+            return ((-x[0], -x[1]), (pre[y, 0, n] - z[0], pre[y, 1, n] - z[1]))
+
+        v, b = lax.fori_loop(0, last, step, (v, b))
+        tm[1, 0, n] = v[0]
+        tm[1, 1, n] = v[1]
+        tm[2, 0, n] = b[0]
+        tm[2, 1, n] = b[1]
+        return carry
+
+    lax.fori_loop(0, F, backward_column, 0)
+
+    def halves(p, q):
+        axis = p.ndim - 1
+        left = lax.broadcasted_iota(jnp.int32, p.shape, axis) < 64
+        return (
+            jnp.where(left, p, pltpu.roll(q, 64, axis)),
+            jnp.where(left, pltpu.roll(p, 64, axis), q),
+        )
+
+    def pack_t(g, carry):
+        at = (g // F) * 32 + lax.rem(g, F) * F
+        d0, d1 = halves(tm[g // F, 0, lax.rem(g, F)], tm[g // F, 1, lax.rem(g, F)])
+        for i in range(F):
+            send_t[pl.ds(at + i, 8, stride=TR), :] = d0[i]
+            send_t[pl.ds(8 * TR + at + i, 8, stride=TR), :] = d1[i]
+        return carry
+
+    lax.fori_loop(0, 3 * F, pack_t, 0)
+
+    def code_transfers(n, carry):
+        encode_blocks(send_t, code_t, 2 * n, 2, 3, 4, 25)
+        return carry
+
+    lax.fori_loop(0, K // 2, code_transfers, 0)
+
+    def t_copy(o):
+        to = wall_peer(o)
+        return remote(code_t.at[to], got_t.at[chip], t_send.at[to], t_recv.at[chip], me_s, to * 2 + core)
+
+    def t_wait(o):
+        frm = wall_peer(o)
+        return remote(code_t.at[frm], got_t.at[frm], t_send.at[frm], t_recv.at[frm], me_s, frm * 2 + core)
+
+    t_local = pltpu.make_async_copy(code_t.at[chip], got_t.at[chip], loc.at[1, 0])
+    t_local.start()
+
+    def start_t(o, carry):
+        t_copy(o).start()
+        return carry
+
+    lax.fori_loop(1, K, start_t, 0)
+
+    filtered(1, 0)
 
     def a_copy(ch, o):
         to = wall_peer(o)
         return remote(
-            send_a.at[a_block(ch, to)], recv_a.at[a_block(ch, chip)], a_send.at[ch, to], a_recv.at[ch, chip], me_s, to * 2 + core
+            code_a.at[ch * K + to], got_a.at[ch * K + chip], a_send.at[ch, to], a_recv.at[ch, chip], me_s, to * 2 + core
         )
 
     def a_wait(ch, o):
         frm = wall_peer(o)
         return remote(
-            send_a.at[a_block(ch, frm)], recv_a.at[a_block(ch, frm)], a_send.at[ch, frm], a_recv.at[ch, frm], me_s, frm * 2 + core
+            code_a.at[ch * K + frm], got_a.at[ch * K + frm], a_send.at[ch, frm], a_recv.at[ch, frm], me_s, frm * 2 + core
         )
 
     def a_local(ch):
-        return pltpu.make_async_copy(send_a.at[a_block(ch, chip)], recv_a.at[a_block(ch, chip)], loc.at[3, ch])
+        return pltpu.make_async_copy(code_a.at[ch * K + chip], got_a.at[ch * K + chip], loc.at[3, ch])
 
     zero = jnp.zeros((F, 8, 128), jnp.float32)
 
@@ -394,6 +421,8 @@
             for i in range(F):
                 send_a[pl.ds(base + g * F + i, 8, stride=AR), :] = d0[i]
                 send_a[pl.ds(base + 8 * AR + g * F + i, 8, stride=AR), :] = d1[i]
+        for n in range(2):
+            encode_blocks(send_a, code_a, ch * K + 8 * n, 8, 1, 3, 20)
         a_local(ch).start()
 
         def start_a(o, carry):
@@ -413,9 +442,15 @@
 
     lax.fori_loop(1, K, wait_t, 0)
 
+    def plain_transfers(n, carry):
+        decode_blocks(got_t, recv_t, 2 * n, 2, 3, 4)
+        return carry
+
+    lax.fori_loop(0, K // 2, plain_transfers, 0)
+
     def expand(k, carry):
         for g in range(3 * F):
-            rows = recv_t[pl.ds(k * TR + g * F, F), :]
+            rows = recv_t[pl.ds(k * TR + (g // F) * 32 + (g % F) * F, F), :]
             left = lax.broadcasted_iota(jnp.int32, rows.shape, 1) < 64
             turned = pltpu.roll(rows, 64, 1)
             te[k, g // F, 0, g % F, 0:F, :] = jnp.where(left, rows, turned)
@@ -438,17 +473,17 @@
     def s_copy(ch, o):
         to = wall_peer(o)
         return remote(
-            send_s.at[a_block(ch, to)], recv_s.at[a_block(ch, chip)], s_send.at[ch, to], s_recv.at[ch, chip], me_s, to * 2 + core
+            code_s.at[ch * K + to], got_s.at[ch * K + chip], s_send.at[ch, to], s_recv.at[ch, chip], me_s, to * 2 + core
         )
 
     def s_wait(ch, o):
         frm = wall_peer(o)
         return remote(
-            send_s.at[a_block(ch, frm)], recv_s.at[a_block(ch, frm)], s_send.at[ch, frm], s_recv.at[ch, frm], me_s, frm * 2 + core
+            code_s.at[ch * K + frm], got_s.at[ch * K + frm], s_send.at[ch, frm], s_recv.at[ch, frm], me_s, frm * 2 + core
         )
 
     def s_local(ch):
-        return pltpu.make_async_copy(send_s.at[a_block(ch, chip)], recv_s.at[a_block(ch, chip)], loc.at[4, ch])
+        return pltpu.make_async_copy(code_s.at[ch * K + chip], got_s.at[ch * K + chip], loc.at[4, ch])
 
     flat = jnp.zeros((F, 128), jnp.float32)
 
@@ -460,6 +495,8 @@
             return carry
 
         lax.fori_loop(1, K, wait_a, 0)
+        for n in range(2):
+            decode_blocks(got_a, recv_a, ch * K + 8 * n, 8, 1, 3)
 
         def forward(k, state):
             base = (ch * K + k) * AR
@@ -482,6 +519,8 @@
             return small(k, 1, state, (qb[k, 0, 0:F, :], qb[k, 1, 0:F, :]))
 
         lax.fori_loop(0, K, backward, (flat, flat))
+        for n in range(2):
+            encode_blocks(send_s, code_s, ch * K + 8 * n, 8, 1, 3, 20)
         s_local(ch).start()
 
         def start_s(o, carry):
@@ -518,6 +557,8 @@
             return carry
 
         lax.fori_loop(1, K, wait_s, 0)
+        for n in range(2):
+            decode_blocks(got_s, recv_s, ch * K + 8 * n, 8, 1, 3)
         base = ch * (K * AR)
 
         def entering(g):
@@ -610,6 +651,9 @@
         vm((K, 3, 2, F, 8, 128), f32),
         vm((2 * K * AR, 128), f32), vm((2 * K * AR, 128), f32),
         vm((2 * K * AR, 128), f32), vm((2 * K * AR, 128), f32),
+        vm((K, 12, 8, 128), bf16), vm((K, 12, 8, 128), bf16),
+        vm((2 * K, 3, 8, 128), bf16), vm((2 * K, 3, 8, 128), bf16),
+        vm((2 * K, 3, 8, 128), bf16), vm((2 * K, 3, 8, 128), bf16),
         vm((2, ROWS, 2, 2, F, 8, 128), f32),
         rows,
         vm((K, 2, 8, 128), f32),

time: 67.4 us -> 58.3 us (0.86)
  Pallas kernels: 64.4 us -> 55.7 us
    pallas_call x1, Pallas kernels: 64.4 us -> 55.7 us  [local(): pl.pallas_call(kernel, out_shape=jax.ShapeDtypeStruct((2 * F, 4, 64, 128)...]
where the time goes in v3:
time: 58.3 us; the launch traced here: 58.2 us
  Pallas kernels  55.7 us (96%)
  local copies, waits for them, and re-layouts  2.52 us (4%)
    pallas_call x1, Pallas kernels, local(): pl.pallas_call(kernel, out_shape=jax.ShapeDtypeStruct((2 * F, 4, 64, 128)...  55.7 us
    unnamed x1, local copies, waits for them, and re-layouts  2.52 us

profile of v3, /device:TPU:1, one launch (start us, length us, event | category | flops | bytes accessed | tf_op | source)
XLA Modules:
  0.0 58.2 jit_solution(10241559724313270538)
XLA Ops:
  0.0 55.7 %shard_map.64 = f32[10,4,64,128]{3,2,1,0:T(8,128)} custom-call(bf16[10,4,64,128]{3,2,1,0:T(8,128)(2,1)} %bitcast.10, f32[5,2,128]{2,1,0:T(2,128)} %bitcast.11, f32[2,128,128]{2,1,0:T(8,128)} %constant.2.clone.table_in, bf16[50,64,128]{2,1,0:T(8,128)(2,1)} %bitcast.7, bf16[50,64,128]{2,1,0:T(8,128)(2,1)} %bitcast.8, bf16[50,64,128]{2,1,0:T(8,128)(2,1)} %bitcast.9), custom_call_target="tpu_custom_call" | custom-call | tf_op jit(solution)/shard_map/pallas_call | solution.py:671
  55.7 2.5 %copy.8 = f32[2,5,4,16,4,128]{5,4,3,2,1,0:T(4,128)} copy(f32[2,5,4,16,4,128]{5,4,3,2,1,0:T(4,128)} %bitcast.6) | data formatting | bytes 2621440

commit v4 on v3

--- a/solution.py
+++ b/solution.py
@@ -75,7 +75,7 @@
 
 def kernel(
     forcing_in, factor_in, table_in, piv_in, low_in, upp_in, out,
-    forcing, factor, table, piv, low, upp, tmp, scales, send_f, recv_f, part_p, part_l, part_u, pf, lf, uf, pre, tm, a_hi, a_lo,
+    forcing, factor, table, piv, low, upp, tmp, line, scales, send_f, recv_f, part_p, part_l, part_u, pf, lf, uf, pre, tm, a_hi, a_lo,
     send_r, driv, send_t, recv_t, te, send_a, recv_a, send_s, recv_s,
     code_t, got_t, code_a, got_a, code_s, got_s, src, sw, qb, resp,
     c_send, c_recv, f_send, f_recv, r_send, r_recv, t_send, t_recv, a_send, a_recv, s_send, s_recv,
@@ -135,8 +135,6 @@
 
     loads[0].wait()
     lax.fori_loop(0, 2 * F, regroup, 0)
-    for copy in loads[1:]:
-        copy.wait()
 
     pl.semaphore_wait(barrier, 2 * S - 1 + K - 1)
 
@@ -160,20 +158,22 @@
     def c_copy(n, ref, part):
         return remote(ref.at[:, pl.ds(other * 32, 32), :], part, c_send.at[n], c_recv.at[n], me_s, partner)
 
-    c_copies = [c_copy(0, low, part_l), c_copy(1, upp, part_u), c_copy(2, piv, part_p)]
+    c_copies = [c_copy(0, low_in, part_l), c_copy(1, upp_in, part_u), c_copy(2, piv_in, part_p)]
+
+    def forcing_out(ch):
+        f_local(ch).start()
+
+        def start_f(o, carry):
+            f_copy(ch, o).start()
+            return carry
+
+        lax.fori_loop(1, S, start_f, 0)
+
+    forcing_out(0)
     for copy in c_copies:
         copy.start()
-
-    def forcing_out(ch):
-        f_local(ch).start()
-
-        def start_f(o, carry):
-            f_copy(ch, o).start()
-            return carry
-
-        lax.fori_loop(1, S, start_f, 0)
-
-    forcing_out(0)
+    for copy in loads[1:]:
+        copy.wait()
 
     def by_row(ref, first, dst, at):
         def step(g, carry):
@@ -190,16 +190,21 @@
     by_row(low, mine, lf, core)
     by_row(upp, mine, uf, core)
     by_row(piv, mine, pf, core)
+    dot = functools.partial(jnp.dot, precision=HI, preferred_element_type=jnp.float32)
+    for f in range(F):
+        line[0, f:f + 1, :] = factor[f, 0:1, :]
+        line[1, f:f + 1, :] = factor[f, 1:2, :]
+    factor_re = line[0, 0:F, :]
+    factor_im = line[1, 0:F, :]
+    first_re = (dot(factor_re, table[0]) + dot(factor_im, table[1])) * (1.0 / 128.0)
+    first_im = (dot(factor_im, table[0]) - dot(factor_re, table[1])) * (1.0 / 128.0)
+    line[0, 0:F, :] = first_re
+    line[1, 0:F, :] = first_im
+
     def build(f, carry):
-        fr = factor[f, 0:1, :]
-        fi = factor[f, 1:2, :]
-        cosine = table[0]
-        sine = table[1]
-        gr = cosine * fr - sine * fi
-        gi = cosine * fi + sine * fr
-        dot = functools.partial(jnp.dot, precision=HI, preferred_element_type=jnp.float32)
-        kr = (dot(gr, cosine) + dot(gi, sine)) * (1.0 / 128.0)
-        ki = (dot(gi, cosine) - dot(gr, sine)) * (1.0 / 128.0)
+        turn = lambda row: pltpu.roll(jnp.broadcast_to(row, (128, 128)), 0, 1, stride=1, stride_axis=0)
+        kr = turn(line[0, pl.ds(f, 1), :])
+        ki = turn(line[1, pl.ds(f, 1), :])
         for rows, cols, block in ((0, 0, kr), (0, 128, -ki), (128, 0, ki), (128, 128, kr)):
             top = block.astype(jnp.bfloat16)
             a_hi[f, rows:rows + 128, cols:cols + 128] = top
@@ -275,12 +280,12 @@
             top = jnp.max(jnp.maximum(jnp.abs(re), jnp.abs(im)), axis=2, keepdims=True)
             scale = jnp.maximum(top * 1.01, 1e-30).astype(jnp.bfloat16).astype(jnp.float32)
             scales[:, :, pl.ds(f, 1), :] = scale
-            codes = jnp.concatenate([encode(re, scale), encode(im, scale)], axis=2)
-            send_r[ch, :, :, f] = codes.astype(jnp.bfloat16)
+            send_r[ch, :, :, f] = encode(re, scale).astype(jnp.bfloat16)
+            send_r[ch, :, :, F + f] = encode(im, scale).astype(jnp.bfloat16)
             return carry
 
         lax.fori_loop(0, F, field, 0)
-        send_r[ch, :, :, F] = jnp.concatenate([scales[...], scales[...]], axis=2).astype(jnp.bfloat16)
+        send_r[ch, :, :, 2 * F] = scales[...].astype(jnp.bfloat16)
         r_local(ch).start()
         r_copy(ch, 0, 1).start()
 
@@ -291,8 +296,6 @@
 
         lax.fori_loop(1, S, start_r, 0)
         return carry
-
-    filtered(0, 0)
 
     def backward_column(n, carry):
         last = ROWS - 1
@@ -312,7 +315,10 @@
         tm[2, 1, n] = b[1]
         return carry
 
-    lax.fori_loop(0, F, backward_column, 0)
+    lax.fori_loop(0, 2, backward_column, 0)
+    filtered(0, 0)
+
+    lax.fori_loop(2, F, backward_column, 0)
 
     def halves(p, q):
         axis = p.ndim - 1
@@ -397,11 +403,9 @@
             base = (y // 4) * S + lax.rem(y, 4)
             drive = []
             for n in range(2):
-                scale = driv[ch, base + 4 * n, F].astype(jnp.float32)
-                parts = [
-                    decode(driv[ch, base + 4 * n, f].astype(jnp.float32), scale[f:f + 1]) for f in range(F)
-                ]
-                drive.append((jnp.stack([x[:8] for x in parts]), jnp.stack([x[8:] for x in parts])))
+                code = driv[ch, base + 4 * n].astype(jnp.float32)
+                scale = jnp.stack([jnp.broadcast_to(code[2 * F, f:f + 1], (8, 128)) for f in range(F)])
+                drive.append((decode(code[:F], scale), decode(code[F:2 * F], scale)))
             source = apply(pf, y, drive)
             put(src.at[ch], y, source)
             state = sub(source, apply(lf, y, state))
@@ -638,6 +642,7 @@
         vm((2 * F, 4, 64, 128), bf16), vm((F, 2, 128), f32), vm((2, 128, 128), f32),
         vm((50, 64, 128), bf16), vm((50, 64, 128), bf16), vm((50, 64, 128), bf16),
         vm((256, 128), f32),
+        vm((2, 8, 128), f32),
         vm((S, 2, 8, 128), f32),
         vm((2, S, F, 2, 16, 128), bf16),
         vm((2, S, F, 2, 16, 128), bf16),
@@ -645,8 +650,8 @@
         coef, coef, coef, coef,
         vm((3, 2, F, F, 8, 128), f32),
         vm((F, 256, 256), bf16), vm((F, 256, 256), bf16),
-        vm((2, S, 2, F + 1, 16, 128), bf16),
-        vm((2, 2 * S, F + 1, 16, 128), bf16),
+        vm((2, S, 2, 2 * F + 1, 8, 128), bf16),
+        vm((2, 2 * S, 2 * F + 1, 8, 128), bf16),
         vm((K * TR, 128), f32), vm((K * TR, 128), f32),
         vm((K, 3, 2, F, 8, 128), f32),
         vm((2 * K * AR, 128), f32), vm((2 * K * AR, 128), f32),
@@ -671,17 +676,22 @@
     out = pl.pallas_call(
         kernel,
         out_shape=jax.ShapeDtypeStruct((2 * F, 4, 64, 128), f32),
-        in_specs=[pl.BlockSpec(memory_space=pl.ANY)] * 6,
+        in_specs=[pl.BlockSpec(memory_space=pltpu.HBM)] * 6,
         out_specs=pl.BlockSpec(memory_space=pl.ANY),
         scratch_shapes=scratch,
         compiler_params=pltpu.CompilerParams(
-            collective_id=0, has_side_effects=True, vmem_limit_bytes=56 << 20
+            collective_id=0, has_side_effects=True, vmem_limit_bytes=34 << 20
         ),
     )(
-        forcing.reshape(2 * F, 4, 64, 128),
-        jnp.swapaxes(span_factor, 0, 1),
-        jnp.asarray(tables()),
-        *flat,
+        *[
+            pltpu.with_memory_space_constraint(x, pltpu.HBM)
+            for x in (
+                forcing.reshape(2 * F, 4, 64, 128),
+                jnp.swapaxes(span_factor, 0, 1),
+                jnp.asarray(tables()),
+                *flat,
+            )
+        ]
     )
     return out.reshape(2, F, 4, 16, 4, 128)
 

time: 58.3 us -> 56.1 us (0.962)
  local copies, waits for them, and re-layouts: 2.52 us -> 1.06 us
  Pallas kernels: 55.7 us -> 54.9 us
    unnamed x1, local copies, waits for them, and re-layouts: 2.52 us -> 1.06 us
    pallas_call x1, Pallas kernels: 55.7 us -> 54.9 us  [local(): pl.pallas_call(kernel, out_shape=jax.ShapeDtypeStruct((2 * F, 4, 64, 128)...]
where the time goes in v4:
time: 56.1 us; the launch traced here: 56 us
  Pallas kernels  54.9 us (98%)
  local copies, waits for them, and re-layouts  1.06 us (2%)
    pallas_call x1, Pallas kernels, local(): pl.pallas_call(kernel, out_shape=jax.ShapeDtypeStruct((2 * F, 4, 64, 128)...  54.9 us

profile of v4, /device:TPU:1, one launch (start us, length us, event | category | flops | bytes accessed | tf_op | source)
XLA Modules:
  0.0 56.0 jit_solution(14492209842270596519)
XLA Ops:
  0.0 54.9 %shard_map.64 = f32[10,4,64,128]{3,2,1,0:T(8,128)S(1)} custom-call(bf16[10,4,64,128]{3,2,1,0:T(8,128)(2,1)} %bitcast.10, f32[5,2,128]{2,1,0:T(2,128)} %bitcast.11, f32[2,128,128]{2,1,0:T(8,128)} %constant.2.clone.table_in, bf16[50,64,128]{2,1,0:T(8,128)(2,1)} %bitcast.7, bf16[50,64,128]{2,1,0:T(8,128)(2,1)} %bitcast.8, bf16[50,64,128]{2,1,0:T(8,128)(2,1)} %bitcast.9), custom_call_target="tpu_custom_call" | custom-call | tf_op jit(solution)/shard_map/pallas_call | solution.py:676
  54.9 1.1 %copy.8 = f32[2,5,4,16,4,128]{5,4,3,2,1,0:T(4,128)} copy(f32[2,5,4,16,4,128]{5,4,3,2,1,0:T(4,128)S(1)} %bitcast.6) | data formatting | bytes 2621440

commit v5 on v4

--- a/solution.py
+++ b/solution.py
@@ -88,11 +88,19 @@
     other = 1 - core
     partner = chip * 2 + other
 
+    def ordered(i, n, first):
+        step = (i + 1) // 2
+        return lax.rem(n // 2 + n + jnp.where(lax.rem(i, 2) == first, step, -step), n)
+
     def span_peer(o):
-        return lax.rem(me_s + o, S)
+        y = lax.rem(me_s // 4 + 1 - lax.rem(o, 2), 2)
+        x = lax.rem(lax.rem(me_s, 4) + ordered(o // 2, 4, 0), 4)
+        return y * 4 + x
 
     def wall_peer(o):
-        return lax.rem(chip + o, K)
+        y = lax.rem(chip // 8 + 1 - o // 8, 2)
+        z = lax.rem(lax.rem(chip, 8) + ordered(lax.rem(o, 8), 8, 1), 8)
+        return y * 8 + z
 
     loads = [
         pltpu.make_async_copy(a, b, load.at[n])
@@ -103,8 +111,7 @@
             )
         )
     ]
-    for copy in loads:
-        copy.start()
+    loads[0].start()
 
     barrier = pltpu.get_barrier_semaphore()
 
@@ -120,9 +127,11 @@
         greet(me_s, wall_peer(o) * 2 + core)
         return carry
 
-    lax.fori_loop(1, S, greet_span, 0)
-    lax.fori_loop(1, K, greet_wall, 0)
+    lax.fori_loop(0, S - 1, greet_span, 0)
     greet(me_s, partner)
+    for copy in loads[1:]:
+        copy.start()
+    lax.fori_loop(0, K - 1, greet_wall, 0)
 
     def regroup(g, carry):
         for col in range(4):
@@ -146,11 +155,11 @@
 
     def f_copy(ch, o):
         to = span_peer(o)
-        return remote(send_f.at[ch, to], recv_f.at[ch, me_s], f_send.at[ch, to], f_recv.at[ch, me_s], to, me_w)
-
-    def f_wait(ch, o):
-        frm = span_peer(o)
-        return remote(send_f.at[ch, frm], recv_f.at[ch, frm], f_send.at[ch, frm], f_recv.at[ch, frm], frm, me_w)
+        return remote(send_f.at[ch, to], recv_f.at[ch, me_s], f_send.at[ch], f_recv.at[ch], to, me_w)
+
+    def f_all(ch):
+        some = pl.ds(0, S - 1)
+        return remote(send_f.at[ch, some], recv_f.at[ch, some], f_send.at[ch], f_recv.at[ch], me_s, partner)
 
     def f_local(ch):
         return pltpu.make_async_copy(send_f.at[ch, me_s], recv_f.at[ch, me_s], loc.at[0, ch])
@@ -167,7 +176,7 @@
             f_copy(ch, o).start()
             return carry
 
-        lax.fori_loop(1, S, start_f, 0)
+        lax.fori_loop(0, S - 1, start_f, 0)
 
     forcing_out(0)
     for copy in c_copies:
@@ -240,33 +249,21 @@
 
     lax.fori_loop(0, F, forward_column, 0)
 
-    def r_copy(ch, o, d):
-        to = span_peer(o)
-        c = core if d == 0 else other
-        slot = core * S + me_s
+    def r_copy(ch, to, c):
         return remote(
-            send_r.at[ch, to, c], driv.at[ch, slot], r_send.at[ch, c * S + to], r_recv.at[ch, slot], to, chip * 2 + c
-        )
-
-    def r_wait(ch, o, d):
-        frm = span_peer(o)
-        c = core if d == 0 else other
-        slot = c * S + frm
-        return remote(
-            send_r.at[ch, frm, c], driv.at[ch, slot], r_send.at[ch, slot], r_recv.at[ch, slot], frm, chip * 2 + c
-        )
+            send_r.at[ch, to * 2 + c], driv.at[ch, core * S + me_s], r_send.at[ch], r_recv.at[ch], to, chip * 2 + c
+        )
+
+    def r_all(ch):
+        some = pl.ds(0, 2 * S - 1)
+        return remote(send_r.at[ch, some], driv.at[ch, some], r_send.at[ch], r_recv.at[ch], me_s, partner)
 
     def r_local(ch):
-        return pltpu.make_async_copy(send_r.at[ch, me_s, core], driv.at[ch, core * S + me_s], loc.at[2, ch])
+        return pltpu.make_async_copy(send_r.at[ch, me_s * 2 + core], driv.at[ch, core * S + me_s], loc.at[2, ch])
 
     def filtered(ch, carry):
         f_local(ch).wait()
-
-        def wait_f(o, carry):
-            f_wait(ch, o).wait_recv()
-            return carry
-
-        lax.fori_loop(1, S, wait_f, 0)
+        f_all(ch).wait_recv()
 
         def field(f, carry):
             rhs = jnp.concatenate(
@@ -275,26 +272,27 @@
             res = jnp.dot(a_hi[f], rhs, preferred_element_type=jnp.float32) + jnp.dot(
                 a_lo[f], rhs, preferred_element_type=jnp.float32
             )
-            re = res[:128].reshape(S, 2, 8, 128)
-            im = res[128:].reshape(S, 2, 8, 128)
-            top = jnp.max(jnp.maximum(jnp.abs(re), jnp.abs(im)), axis=2, keepdims=True)
+            re = res[:128].reshape(2 * S, 8, 128)
+            im = res[128:].reshape(2 * S, 8, 128)
+            top = jnp.max(jnp.maximum(jnp.abs(re), jnp.abs(im)), axis=1, keepdims=True)
             scale = jnp.maximum(top * 1.01, 1e-30).astype(jnp.bfloat16).astype(jnp.float32)
-            scales[:, :, pl.ds(f, 1), :] = scale
-            send_r[ch, :, :, f] = encode(re, scale).astype(jnp.bfloat16)
-            send_r[ch, :, :, F + f] = encode(im, scale).astype(jnp.bfloat16)
+            scales[:, pl.ds(f, 1), :] = scale
+            send_r[ch, :, f] = encode(re, scale).astype(jnp.bfloat16)
+            send_r[ch, :, F + f] = encode(im, scale).astype(jnp.bfloat16)
             return carry
 
         lax.fori_loop(0, F, field, 0)
-        send_r[ch, :, :, 2 * F] = scales[...].astype(jnp.bfloat16)
+        send_r[ch, :, 2 * F] = scales[...].astype(jnp.bfloat16)
         r_local(ch).start()
-        r_copy(ch, 0, 1).start()
 
         def start_r(o, carry):
-            r_copy(ch, o, 0).start()
-            r_copy(ch, o, 1).start()
+            to = span_peer(o)
+            r_copy(ch, to, core).start()
+            r_copy(ch, to, other).start()
             return carry
 
-        lax.fori_loop(1, S, start_r, 0)
+        lax.fori_loop(0, S - 1, start_r, 0)
+        r_copy(ch, me_s, other).start()
         return carry
 
     def backward_column(n, carry):
@@ -346,11 +344,11 @@
 
     def t_copy(o):
         to = wall_peer(o)
-        return remote(code_t.at[to], got_t.at[chip], t_send.at[to], t_recv.at[chip], me_s, to * 2 + core)
-
-    def t_wait(o):
-        frm = wall_peer(o)
-        return remote(code_t.at[frm], got_t.at[frm], t_send.at[frm], t_recv.at[frm], me_s, frm * 2 + core)
+        return remote(code_t.at[to], got_t.at[chip], t_send.at[0], t_recv.at[0], me_s, to * 2 + core)
+
+    def t_all():
+        some = pl.ds(0, K - 1)
+        return remote(code_t.at[some], got_t.at[some], t_send.at[0], t_recv.at[0], me_s, partner)
 
     t_local = pltpu.make_async_copy(code_t.at[chip], got_t.at[chip], loc.at[1, 0])
     t_local.start()
@@ -359,21 +357,19 @@
         t_copy(o).start()
         return carry
 
-    lax.fori_loop(1, K, start_t, 0)
+    lax.fori_loop(0, K - 1, start_t, 0)
 
     filtered(1, 0)
 
     def a_copy(ch, o):
         to = wall_peer(o)
         return remote(
-            code_a.at[ch * K + to], got_a.at[ch * K + chip], a_send.at[ch, to], a_recv.at[ch, chip], me_s, to * 2 + core
-        )
-
-    def a_wait(ch, o):
-        frm = wall_peer(o)
-        return remote(
-            code_a.at[ch * K + frm], got_a.at[ch * K + frm], a_send.at[ch, frm], a_recv.at[ch, frm], me_s, frm * 2 + core
-        )
+            code_a.at[ch * K + to], got_a.at[ch * K + chip], a_send.at[ch], a_recv.at[ch], me_s, to * 2 + core
+        )
+
+    def a_all(ch):
+        some = pl.ds(ch * K, K - 1)
+        return remote(code_a.at[some], got_a.at[some], a_send.at[ch], a_recv.at[ch], me_s, partner)
 
     def a_local(ch):
         return pltpu.make_async_copy(code_a.at[ch * K + chip], got_a.at[ch * K + chip], loc.at[3, ch])
@@ -390,14 +386,7 @@
 
     def local_solve(ch, carry):
         r_local(ch).wait()
-        r_wait(ch, 0, 1).wait_recv()
-
-        def wait_r(o, carry):
-            r_wait(ch, o, 0).wait_recv()
-            r_wait(ch, o, 1).wait_recv()
-            return carry
-
-        lax.fori_loop(1, S, wait_r, 0)
+        r_all(ch).wait_recv()
 
         def forward(y, state):
             base = (y // 4) * S + lax.rem(y, 4)
@@ -433,18 +422,13 @@
             a_copy(ch, o).start()
             return carry
 
-        lax.fori_loop(1, K, start_a, 0)
+        lax.fori_loop(0, K - 1, start_a, 0)
         return carry
 
     lax.fori_loop(0, 2, local_solve, 0)
 
     t_local.wait()
-
-    def wait_t(o, carry):
-        t_wait(o).wait_recv()
-        return carry
-
-    lax.fori_loop(1, K, wait_t, 0)
+    t_all().wait_recv()
 
     def plain_transfers(n, carry):
         decode_blocks(got_t, recv_t, 2 * n, 2, 3, 4)
@@ -477,14 +461,12 @@
     def s_copy(ch, o):
         to = wall_peer(o)
         return remote(
-            code_s.at[ch * K + to], got_s.at[ch * K + chip], s_send.at[ch, to], s_recv.at[ch, chip], me_s, to * 2 + core
-        )
-
-    def s_wait(ch, o):
-        frm = wall_peer(o)
-        return remote(
-            code_s.at[ch * K + frm], got_s.at[ch * K + frm], s_send.at[ch, frm], s_recv.at[ch, frm], me_s, frm * 2 + core
-        )
+            code_s.at[ch * K + to], got_s.at[ch * K + chip], s_send.at[ch], s_recv.at[ch], me_s, to * 2 + core
+        )
+
+    def s_all(ch):
+        some = pl.ds(ch * K, K - 1)
+        return remote(code_s.at[some], got_s.at[some], s_send.at[ch], s_recv.at[ch], me_s, partner)
 
     def s_local(ch):
         return pltpu.make_async_copy(code_s.at[ch * K + chip], got_s.at[ch * K + chip], loc.at[4, ch])
@@ -493,12 +475,7 @@
 
     def owner_scan(ch, carry):
         a_local(ch).wait()
-
-        def wait_a(o, carry):
-            a_wait(ch, o).wait_recv()
-            return carry
-
-        lax.fori_loop(1, K, wait_a, 0)
+        a_all(ch).wait_recv()
         for n in range(2):
             decode_blocks(got_a, recv_a, ch * K + 8 * n, 8, 1, 3)
 
@@ -531,7 +508,7 @@
             s_copy(ch, o).start()
             return carry
 
-        lax.fori_loop(1, K, start_s, 0)
+        lax.fori_loop(0, K - 1, start_s, 0)
         return carry
 
     lax.fori_loop(0, 2, owner_scan, 0)
@@ -555,12 +532,7 @@
 
     def final(ch, carry):
         s_local(ch).wait()
-
-        def wait_s(o, carry):
-            s_wait(ch, o).wait_recv()
-            return carry
-
-        lax.fori_loop(1, K, wait_s, 0)
+        s_all(ch).wait_recv()
         for n in range(2):
             decode_blocks(got_s, recv_s, ch * K + 8 * n, 8, 1, 3)
         base = ch * (K * AR)
@@ -602,27 +574,11 @@
         o_local(ch).wait()
         o_wait(ch).wait_recv()
         o_copy(ch).wait_send()
-        r_copy(ch, 0, 1).wait_send()
-
-        def end_span(o, carry):
-            f_copy(ch, o).wait_send()
-            r_copy(ch, o, 0).wait_send()
-            r_copy(ch, o, 1).wait_send()
-            return carry
-
-        def end_wall(o, carry):
-            a_copy(ch, o).wait_send()
-            s_copy(ch, o).wait_send()
-            return carry
-
-        lax.fori_loop(1, S, end_span, 0)
-        lax.fori_loop(1, K, end_wall, 0)
-
-    def end_t(o, carry):
-        t_copy(o).wait_send()
-        return carry
-
-    lax.fori_loop(1, K, end_t, 0)
+        f_all(ch).wait_send()
+        r_all(ch).wait_send()
+        a_all(ch).wait_send()
+        s_all(ch).wait_send()
+    t_all().wait_send()
 
 
 def tables():
@@ -643,14 +599,14 @@
         vm((50, 64, 128), bf16), vm((50, 64, 128), bf16), vm((50, 64, 128), bf16),
         vm((256, 128), f32),
         vm((2, 8, 128), f32),
-        vm((S, 2, 8, 128), f32),
+        vm((2 * S, 8, 128), f32),
         vm((2, S, F, 2, 16, 128), bf16),
         vm((2, S, F, 2, 16, 128), bf16),
         vm((50, 32, 128), bf16), vm((50, 32, 128), bf16), vm((50, 32, 128), bf16),
         coef, coef, coef, coef,
         vm((3, 2, F, F, 8, 128), f32),
         vm((F, 256, 256), bf16), vm((F, 256, 256), bf16),
-        vm((2, S, 2, 2 * F + 1, 8, 128), bf16),
+        vm((2, 2 * S, 2 * F + 1, 8, 128), bf16),
         vm((2, 2 * S, 2 * F + 1, 8, 128), bf16),
         vm((K * TR, 128), f32), vm((K * TR, 128), f32),
         vm((K, 3, 2, F, 8, 128), f32),
@@ -664,11 +620,11 @@
         vm((K, 2, 8, 128), f32),
         vm((2, 2, 2 * F, 2, 32, 128), f32),
         dma((3,)), dma((3,)),
-        dma((2, S)), dma((2, S)),
-        dma((2, 2 * S)), dma((2, 2 * S)),
-        dma((K,)), dma((K,)),
-        dma((2, K)), dma((2, K)),
-        dma((2, K)), dma((2, K)),
+        dma((2,)), dma((2,)),
+        dma((2,)), dma((2,)),
+        dma((1,)), dma((1,)),
+        dma((2,)), dma((2,)),
+        dma((2,)), dma((2,)),
         dma((2,)), dma((2,)),
         dma((6, 2)),
         dma((6,)),

time: 56.1 us -> 53.3 us (0.950)
  Pallas kernels: 54.9 us -> 52.2 us
    pallas_call x1, Pallas kernels: 54.9 us -> 52.2 us  [local(): pl.pallas_call(kernel, out_shape=jax.ShapeDtypeStruct((2 * F, 4, 64, 128)...]
where the time goes in v5:
time: 53.3 us; the launch traced here: 53.2 us
  Pallas kernels  52.2 us (98%)
  local copies, waits for them, and re-layouts  1.06 us (2%)
    pallas_call x1, Pallas kernels, local(): pl.pallas_call(kernel, out_shape=jax.ShapeDtypeStruct((2 * F, 4, 64, 128)...  52.2 us

profile of v5, /device:TPU:1, one launch (start us, length us, event | category | flops | bytes accessed | tf_op | source)
XLA Modules:
  0.0 53.2 jit_solution(11007818354053995697)
XLA Ops:
  0.0 52.2 %shard_map.64 = f32[10,4,64,128]{3,2,1,0:T(8,128)S(1)} custom-call(bf16[10,4,64,128]{3,2,1,0:T(8,128)(2,1)} %bitcast.10, f32[5,2,128]{2,1,0:T(2,128)} %bitcast.11, f32[2,128,128]{2,1,0:T(8,128)} %constant.2.clone.table_in, bf16[50,64,128]{2,1,0:T(8,128)(2,1)} %bitcast.7, bf16[50,64,128]{2,1,0:T(8,128)(2,1)} %bitcast.8, bf16[50,64,128]{2,1,0:T(8,128)(2,1)} %bitcast.9), custom_call_target="tpu_custom_call" | custom-call | tf_op jit(solution)/shard_map/pallas_call | solution.py:632
  52.2 1.1 %copy.8 = f32[2,5,4,16,4,128]{5,4,3,2,1,0:T(4,128)} copy(f32[2,5,4,16,4,128]{5,4,3,2,1,0:T(4,128)S(1)} %bitcast.6) | data formatting | bytes 2621440

commit v6 on v5

--- a/solution.py
+++ b/solution.py
@@ -14,7 +14,7 @@
 S = 8
 K = 16
 ROWS = 8
-TR = 96
+TR = 80
 AR = 24
 HI = lax.Precision.HIGHEST
 LEVELS = 29900.0
@@ -55,18 +55,44 @@
     dst[pl.ds(pl.multiple_of(first * rows, 8), count * rows), :] = x.reshape(count * rows, 128)
 
 
+def by_matrix(place, values):
+    return jnp.where(place < 25, values[0], jnp.where(place < 50, values[1], values[2]))
+
+
+def encode_transfers(src, dst, first, count):
+    x = src[pl.ds(pl.multiple_of(first * TR, 8), count * TR), :].reshape(count, TR // 8, 8, 128)
+    place = lax.broadcasted_iota(jnp.int32, x.shape, 1) * 8 + lax.broadcasted_iota(jnp.int32, x.shape, 2)
+    size = jnp.abs(x)
+    scales = []
+    for m in range(3):
+        own = jnp.where((place >= 25 * m) & (place < 25 * m + 25), size, 0.0)
+        top = jnp.max(jnp.max(own, axis=1, keepdims=True), axis=2, keepdims=True)
+        scales.append(jnp.maximum(top * 1.01, 1e-30).astype(jnp.bfloat16).astype(jnp.float32))
+    good = place < 75
+    code = encode(jnp.where(good, x, 0.0), by_matrix(place, scales))
+    tail = jnp.where(place == 76, scales[1], jnp.where(place == 77, scales[2], scales[0]))
+    dst[pl.ds(first, count)] = jnp.where(good, code, tail).astype(jnp.bfloat16)
+
+
+def decode_transfers(src, dst, first, count):
+    code = src[pl.ds(first, count)].astype(jnp.float32)
+    place = lax.broadcasted_iota(jnp.int32, code.shape, 1) * 8 + lax.broadcasted_iota(jnp.int32, code.shape, 2)
+    scale = by_matrix(place, [code[:, 9:, 3 + m:4 + m, :] for m in range(3)])
+    dst[pl.ds(pl.multiple_of(first * TR, 8), count * TR), :] = decode(code, scale).reshape(count * TR, 128)
+
+
 def apply(coef, y, vectors):
     out = [None] * len(vectors)
     for j in range(F):
-        cr = coef[y, 0, j]
-        ci = coef[y, 1, j]
+        c = coef[y, 0, j]
+        d = coef[y, 1, j]
+        e = coef[y, 2, j]
         for n, (vr, vi) in enumerate(vectors):
-            xr = vr[j][None]
-            xi = vi[j][None]
-            re = cr * xr - ci * xi
-            im = cr * xi + ci * xr
-            out[n] = (re, im) if out[n] is None else (out[n][0] + re, out[n][1] + im)
-    return out
+            xr = vr[j]
+            xi = vi[j]
+            p = (c * (xr + xi)[None], d * xr[None], e * xi[None])
+            out[n] = p if out[n] is None else tuple(a + b for a, b in zip(out[n], p))
+    return [(p[0] - p[2], p[0] + p[1]) for p in out]
 
 
 def sub(a, b):
@@ -133,17 +159,20 @@
         copy.start()
     lax.fori_loop(0, K - 1, greet_wall, 0)
 
-    def regroup(g, carry):
-        for col in range(4):
-            tmp[pl.ds(col * 64, 64), :] = forcing[g, col].astype(jnp.float32)
-        for col in range(4):
-            for y in range(4):
-                piece = tmp[pl.ds(col * 64 + y, 16, stride=4), :].astype(jnp.bfloat16)
-                send_f[col // 2, (col % 2) * 4 + y, lax.rem(g, F), g // F] = piece
-        return carry
+    def regroup(ch):
+        def step(g, carry):
+            for n in range(2):
+                tmp[pl.ds(n * 64, 64), :] = forcing[g, 2 * ch + n].astype(jnp.float32)
+            for n in range(2):
+                for y in range(4):
+                    piece = tmp[pl.ds(n * 64 + y, 16, stride=4), :].astype(jnp.bfloat16)
+                    send_f[ch, n * 4 + y, lax.rem(g, F), g // F] = piece
+            return carry
+
+        lax.fori_loop(0, 2 * F, step, 0)
 
     loads[0].wait()
-    lax.fori_loop(0, 2 * F, regroup, 0)
+    regroup(0)
 
     pl.semaphore_wait(barrier, 2 * S - 1 + K - 1)
 
@@ -181,24 +210,29 @@
     forcing_out(0)
     for copy in c_copies:
         copy.start()
+    regroup(1)
     for copy in loads[1:]:
         copy.wait()
 
     def by_row(ref, first, dst, at):
-        def step(g, carry):
-            for j in range(F):
-                tmp[pl.ds(j * 32, 32), :] = ref[g * F + j, pl.ds(first, 32), :].astype(jnp.float32)
+        def step(i, carry):
+            for ri in range(2):
+                for j in range(F):
+                    tmp[pl.ds((ri * F + j) * 32, 32), :] = ref[(ri * F + i) * F + j, pl.ds(first, 32), :].astype(jnp.float32)
             for j in range(F):
                 for y in range(4):
-                    dst[at * 4 + y, g // F, j, lax.rem(g, F)] = tmp[pl.ds(j * 32 + y, 8, stride=4), :]
+                    re = tmp[pl.ds(j * 32 + y, 8, stride=4), :]
+                    im = tmp[pl.ds((F + j) * 32 + y, 8, stride=4), :]
+                    dst[at * 4 + y, 0, j, i] = re
+                    dst[at * 4 + y, 1, j, i] = im - re
+                    dst[at * 4 + y, 2, j, i] = im + re
             return carry
 
-        lax.fori_loop(0, 2 * F, step, 0)
+        lax.fori_loop(0, F, step, 0)
 
     mine = pl.multiple_of(core * 32, 32)
     by_row(low, mine, lf, core)
     by_row(upp, mine, uf, core)
-    by_row(piv, mine, pf, core)
     dot = functools.partial(jnp.dot, precision=HI, preferred_element_type=jnp.float32)
     for f in range(F):
         line[0, f:f + 1, :] = factor[f, 0:1, :]
@@ -227,27 +261,30 @@
     by_row(part_l, 0, lf, other)
     c_copies[1].wait()
     by_row(part_u, 0, uf, other)
-    c_copies[2].wait()
-    by_row(part_p, 0, pf, other)
-
-    def forward_column(n, carry):
-        v = (-lf[0, 0, n], -lf[0, 1, n])
-        pre[0, 0, n] = v[0]
-        pre[0, 1, n] = v[1]
-
-        def step(y, v):
-            w = apply(lf, y, [v])[0]
-            w = (-w[0], -w[1])
-            pre[y, 0, n] = w[0]
-            pre[y, 1, n] = w[1]
-            return w
-
-        v = lax.fori_loop(1, ROWS, step, v)
-        tm[0, 0, n] = v[0]
-        tm[0, 1, n] = v[1]
-        return carry
-
-    lax.fori_loop(0, F, forward_column, 0)
+
+    def forward_columns(columns):
+        state = [(-lf[0, 0, n], -(lf[0, 0, n] + lf[0, 1, n])) for n in columns]
+        for n, v in zip(columns, state):
+            pre[0, 0, n] = v[0]
+            pre[0, 1, n] = v[1]
+
+        def step(y, state):
+            state = [(-w[0], -w[1]) for w in apply(lf, y, state)]
+            for n, v in zip(columns, state):
+                pre[y, 0, n] = v[0]
+                pre[y, 1, n] = v[1]
+            return state
+
+        for n, v in zip(columns, lax.fori_loop(1, ROWS, step, state)):
+            tm[0, 0, n] = v[0]
+            tm[0, 1, n] = v[1]
+
+    def forward_pair(p, carry):
+        forward_columns([2 * p, 2 * p + 1])
+        return carry
+
+    lax.fori_loop(0, 2, forward_pair, 0)
+    forward_columns([4])
 
     def r_copy(ch, to, c):
         return remote(
@@ -297,7 +334,7 @@
 
     def backward_column(n, carry):
         last = ROWS - 1
-        v = (-uf[last, 0, n], -uf[last, 1, n])
+        v = (-uf[last, 0, n], -(uf[last, 0, n] + uf[last, 1, n]))
         b = (pre[last, 0, n], pre[last, 1, n])
 
         def step(t, state):
@@ -313,10 +350,11 @@
         tm[2, 1, n] = b[1]
         return carry
 
-    lax.fori_loop(0, 2, backward_column, 0)
+
+    lax.fori_loop(0, 3, backward_column, 0)
     filtered(0, 0)
-
-    lax.fori_loop(2, F, backward_column, 0)
+    filtered(1, 0)
+    lax.fori_loop(3, F, backward_column, 0)
 
     def halves(p, q):
         axis = p.ndim - 1
@@ -327,7 +365,7 @@
         )
 
     def pack_t(g, carry):
-        at = (g // F) * 32 + lax.rem(g, F) * F
+        at = g * F
         d0, d1 = halves(tm[g // F, 0, lax.rem(g, F)], tm[g // F, 1, lax.rem(g, F)])
         for i in range(F):
             send_t[pl.ds(at + i, 8, stride=TR), :] = d0[i]
@@ -337,7 +375,7 @@
     lax.fori_loop(0, 3 * F, pack_t, 0)
 
     def code_transfers(n, carry):
-        encode_blocks(send_t, code_t, 2 * n, 2, 3, 4, 25)
+        encode_transfers(send_t, code_t, 2 * n, 2)
         return carry
 
     lax.fori_loop(0, K // 2, code_transfers, 0)
@@ -359,7 +397,9 @@
 
     lax.fori_loop(0, K - 1, start_t, 0)
 
-    filtered(1, 0)
+    by_row(piv, mine, pf, core)
+    c_copies[2].wait()
+    by_row(part_p, 0, pf, other)
 
     def a_copy(ch, o):
         to = wall_peer(o)
@@ -425,20 +465,22 @@
         lax.fori_loop(0, K - 1, start_a, 0)
         return carry
 
-    lax.fori_loop(0, 2, local_solve, 0)
+    local_solve(0, 0)
+
+    local_solve(1, 0)
 
     t_local.wait()
     t_all().wait_recv()
 
     def plain_transfers(n, carry):
-        decode_blocks(got_t, recv_t, 2 * n, 2, 3, 4)
+        decode_transfers(got_t, recv_t, 2 * n, 2)
         return carry
 
     lax.fori_loop(0, K // 2, plain_transfers, 0)
 
     def expand(k, carry):
         for g in range(3 * F):
-            rows = recv_t[pl.ds(k * TR + (g // F) * 32 + (g % F) * F, F), :]
+            rows = recv_t[pl.ds(k * TR + g * F, F), :]
             left = lax.broadcasted_iota(jnp.int32, rows.shape, 1) < 64
             turned = pltpu.roll(rows, 64, 1)
             te[k, g // F, 0, g % F, 0:F, :] = jnp.where(left, rows, turned)
@@ -592,18 +634,18 @@
     dma = pltpu.SemaphoreType.DMA
     vm = pltpu.VMEM
     flat = [x.reshape(50, 64, 128) for x in (pivot_inverse, step_lower, step_upper)]
-    coef = vm((ROWS, 2, F, F, 8, 128), f32)
+    coef = vm((ROWS, 3, F, F, 8, 128), f32)
     rows = vm((ROWS, 2, 2, F, 8, 128), f32)
     scratch = [
         vm((2 * F, 4, 64, 128), bf16), vm((F, 2, 128), f32), vm((2, 128, 128), f32),
         vm((50, 64, 128), bf16), vm((50, 64, 128), bf16), vm((50, 64, 128), bf16),
-        vm((256, 128), f32),
+        vm((2 * F * 32, 128), f32),
         vm((2, 8, 128), f32),
         vm((2 * S, 8, 128), f32),
         vm((2, S, F, 2, 16, 128), bf16),
         vm((2, S, F, 2, 16, 128), bf16),
         vm((50, 32, 128), bf16), vm((50, 32, 128), bf16), vm((50, 32, 128), bf16),
-        coef, coef, coef, coef,
+        coef, coef, coef, vm((ROWS, 2, F, F, 8, 128), f32),
         vm((3, 2, F, F, 8, 128), f32),
         vm((F, 256, 256), bf16), vm((F, 256, 256), bf16),
         vm((2, 2 * S, 2 * F + 1, 8, 128), bf16),
@@ -612,7 +654,7 @@
         vm((K, 3, 2, F, 8, 128), f32),
         vm((2 * K * AR, 128), f32), vm((2 * K * AR, 128), f32),
         vm((2 * K * AR, 128), f32), vm((2 * K * AR, 128), f32),
-        vm((K, 12, 8, 128), bf16), vm((K, 12, 8, 128), bf16),
+        vm((K, TR // 8, 8, 128), bf16), vm((K, TR // 8, 8, 128), bf16),
         vm((2 * K, 3, 8, 128), bf16), vm((2 * K, 3, 8, 128), bf16),
         vm((2 * K, 3, 8, 128), bf16), vm((2 * K, 3, 8, 128), bf16),
         vm((2, ROWS, 2, 2, F, 8, 128), f32),

time: 53.3 us -> 49.4 us (0.927)
  Pallas kernels: 52.2 us -> 48.3 us
    pallas_call x1, Pallas kernels: 52.2 us -> 48.3 us  [local(): pl.pallas_call(kernel, out_shape=jax.ShapeDtypeStruct((2 * F, 4, 64, 128)...]
where the time goes in v6:
time: 49.4 us
  Pallas kernels  48.3 us (98%)
  local copies, waits for them, and re-layouts  1.06 us (2%)
    pallas_call x1, Pallas kernels, local(): pl.pallas_call(kernel, out_shape=jax.ShapeDtypeStruct((2 * F, 4, 64, 128)...  48.3 us
    unnamed x1, local copies, waits for them, and re-layouts  1.06 us

profile of v6, /device:TPU:1, one launch (start us, length us, event | category | flops | bytes accessed | tf_op | source)
XLA Modules:
  0.0 49.4 jit_solution(9744768374293472562)
XLA Ops:
  0.0 48.3 %shard_map.64 = f32[10,4,64,128]{3,2,1,0:T(8,128)S(1)} custom-call(bf16[10,4,64,128]{3,2,1,0:T(8,128)(2,1)} %bitcast.10, f32[5,2,128]{2,1,0:T(2,128)} %bitcast.11, f32[2,128,128]{2,1,0:T(8,128)} %constant.2.clone.table_in, bf16[50,64,128]{2,1,0:T(8,128)(2,1)} %bitcast.7, bf16[50,64,128]{2,1,0:T(8,128)(2,1)} %bitcast.8, bf16[50,64,128]{2,1,0:T(8,128)(2,1)} %bitcast.9), custom_call_target="tpu_custom_call" | custom-call | tf_op jit(solution)/shard_map/pallas_call | solution.py:674
  48.3 1.1 %copy.8 = f32[2,5,4,16,4,128]{5,4,3,2,1,0:T(4,128)} copy(f32[2,5,4,16,4,128]{5,4,3,2,1,0:T(4,128)S(1)} %bitcast.6) | data formatting | bytes 2621440

commit v7 on v6

--- a/solution.py
+++ b/solution.py
@@ -351,10 +351,10 @@
         return carry
 
 
-    lax.fori_loop(0, 3, backward_column, 0)
+    lax.fori_loop(0, 4, backward_column, 0)
     filtered(0, 0)
     filtered(1, 0)
-    lax.fori_loop(3, F, backward_column, 0)
+    lax.fori_loop(4, F, backward_column, 0)
 
     def halves(p, q):
         axis = p.ndim - 1

time: 49.4 us -> 49.8 us (level)
  no operation moved by 1% of the time
where the time goes in v7:
time: 49.8 us; the launch traced here: 49.7 us
  Pallas kernels  48.7 us (98%)
  local copies, waits for them, and re-layouts  1.06 us (2%)
    pallas_call x1, Pallas kernels, local(): pl.pallas_call(kernel, out_shape=jax.ShapeDtypeStruct((2 * F, 4, 64, 128)...  48.7 us
    unnamed x1, local copies, waits for them, and re-layouts  1.06 us

profile of v7, /device:TPU:1, one launch (start us, length us, event | category | flops | bytes accessed | tf_op | source)
XLA Modules:
  0.0 49.7 jit_solution(1089451589235577132)
XLA Ops:
  0.0 48.7 %shard_map.64 = f32[10,4,64,128]{3,2,1,0:T(8,128)S(1)} custom-call(bf16[10,4,64,128]{3,2,1,0:T(8,128)(2,1)} %bitcast.10, f32[5,2,128]{2,1,0:T(2,128)} %bitcast.11, f32[2,128,128]{2,1,0:T(8,128)} %constant.2.clone.table_in, bf16[50,64,128]{2,1,0:T(8,128)(2,1)} %bitcast.7, bf16[50,64,128]{2,1,0:T(8,128)(2,1)} %bitcast.8, bf16[50,64,128]{2,1,0:T(8,128)(2,1)} %bitcast.9), custom_call_target="tpu_custom_call" | custom-call | tf_op jit(solution)/shard_map/pallas_call | solution.py:674
  48.7 1.1 %copy.8 = f32[2,5,4,16,4,128]{5,4,3,2,1,0:T(4,128)} copy(f32[2,5,4,16,4,128]{5,4,3,2,1,0:T(4,128)S(1)} %bitcast.6) | data formatting | bytes 2621440
